TPU v7x, 32 devices: a whole 2x2x4 slice. The times are simulated.
32 devices in a mesh: dp: 8 (over z, y), tensor: 4 (over x, core).
Axes of the slice: x: 2, y: 2, z: 4, core: 2. Of those that a mesh axis runs over, the one named last changes fastest.
Arguments:
- q_nope: bfloat16 [32, 2, 128, 128], P('dp', None, 'tensor'), parts along dimension 0, may hold values from -6 to 6
- q_rope: bfloat16 [32, 2, 128, 64], P('dp', None, 'tensor'), parts along dimension 0, may hold values from -8 to 8
- w_uk: bfloat16 [128, 128, 512], P('tensor'), may hold values from -0.5 to 0.5
- w_uv: bfloat16 [128, 512, 128], P('tensor'), may hold values from -0.25 to 0.25
- cache_latent: bfloat16 [32, 8192, 512], P('dp', 'tensor'), parts along dimension 0, may hold values from -4 to 4
- cache_rope: bfloat16 [32, 64, 8192], P('dp', None, 'tensor'), parts along dimension 0, may hold values from -14 to 14
- scale_pool: float32 [5, 2048], P(None, ('dp', 'tensor')), parts along dimension 1, may hold values from 0.3 to 3
- block_index: int32 [32, 64], P('dp', 'tensor'), parts along dimension 0, may hold values from 0 to 255, as said below
- lengths: int32 [32], P('dp'), parts along dimension 0, may hold values from 2048 to 8192, as said below
Outputs:
- head_outputs: bfloat16 [32, 2, 128, 128], P('dp', None, 'tensor'), parts along dimension 0
There are 8 independent parts, one for each index of `dp`. A program takes and returns all parts, laid end to end along the dimension named above; an argument that names none is the same for every part. Nothing has to cross between parts.
Inputs may be any that keep to these rules, and one draw needn't show every extreme that they name: `block_index`: every column of the scale table is named by exactly one cache block of the group. `lengths`: in a group of two or more requests, one request is shorter than 4096 and the others are at least 4096 long.
All inputs are finite; a program needn't handle non-finite values.
Results may differ from a plain program's by a relative error of at most 0.012.
Values may be sent and summed in bfloat16 or wider, within the bound.
No kernel may reach another device: no remote copies, remote signals or barrier semaphores. Data moves between devices by JAX's collectives and lax.ppermute only.
A program may use at most 128 MiB of HBM per device.

v0:
```python
import functools
import math

import jax
import jax.numpy as jnp
from jax import lax
from jax.experimental import pallas as pl
from jax.experimental.pallas import tpu as pltpu
from jax.sharding import PartitionSpec as P


f32, bf16 = jnp.float32, jnp.bfloat16
masked_score = -1e30
VMEM = pl.BlockSpec(memory_space=pltpu.VMEM)
SMEM = pl.BlockSpec(memory_space=pltpu.SMEM)
HBM = pl.BlockSpec(memory_space=pltpu.HBM)


def prepare_kernel(
    first, pieces, index_ref, scale_ref, latent_hbm, rope_hbm, key_ref, turned_ref, latent, rope, latent_sem, rope_sem
):
    requests, span, width = latent.shape
    blocks = index_ref.shape[1]
    shards, groups, per = scale_ref.shape
    block = span // blocks
    lanes = width // (groups - 1)
    me = lax.axis_index("tensor")
    chips = shards // 2
    step = blocks // pieces

    def latent_copy(r, p):
        at = pl.ds(p * step * block, step * block)
        return pltpu.make_async_copy(
            latent_hbm.at[first + r, at], latent.at[r, at], latent_sem.at[r, p]
        )

    def rope_copy(r):
        return pltpu.make_async_copy(rope_hbm.at[first + r], rope.at[r], rope_sem.at[r])

    for r in range(requests):
        rope_copy(r).start()
        for p in range(pieces):
            latent_copy(r, p).start()

    for r in range(requests):
        rope_copy(r).wait()
        for p in range(pieces):
            latent_copy(r, p).wait()
            for b in range(p * step, (p + 1) * step):
                column = index_ref[first + r, b]
                owner, place = lax.div(column, per), lax.rem(column, per)
                turn = lax.rem(me // 2 - owner // 2 + chips, chips)
                other = (me - owner) & 1
                shard = jnp.where(turn == 0, other, turn + 1 + other * (chips - 1))
                at = pl.ds(b * block, block)
                for g in range(groups - 1):
                    part = pl.ds(g * lanes, lanes)
                    scaled = (latent[r, at, part].astype(f32) * scale_ref[shard, g, place]).astype(bf16)
                    key_ref[r, at, part] = scaled
                    turned_ref[r, part, at] = scaled.T
                turned_ref[r, pl.ds(width, rope.shape[1]), at] = (
                    rope[r, :, at].astype(f32) * scale_ref[shard, groups - 1, place]
                ).astype(bf16)


def prepare(first, requests, index, scales, latent, rope):
    span, width = latent.shape[1:]
    depth = rope.shape[1]
    pieces = 1
    return pl.pallas_call(
        functools.partial(prepare_kernel, first, pieces),
        in_specs=[SMEM, SMEM, HBM, HBM],
        out_specs=[VMEM, VMEM],
        out_shape=[
            jax.ShapeDtypeStruct((requests, span, width), bf16),
            jax.ShapeDtypeStruct((requests, width + depth, span), bf16),
        ],
        scratch_shapes=[
            pltpu.VMEM((requests, span, width), bf16),
            pltpu.VMEM((requests, depth, span), bf16),
            pltpu.SemaphoreType.DMA((requests, pieces)),
            pltpu.SemaphoreType.DMA((requests,)),
        ],
        compiler_params=pltpu.CompilerParams(vmem_limit_bytes=12 << 20),
        cost_estimate=pl.CostEstimate(flops=20_000_000, bytes_accessed=20_000_000, transcendentals=0),
        name="prepare",
    )(
        index,
        scales,
        pltpu.with_memory_space_constraint(latent, pltpu.HBM),
        pltpu.with_memory_space_constraint(rope, pltpu.HBM),
    )


def attend_kernel(
    first, tokens, factor, length_ref, qa_ref, qb_ref, ra_ref, rb_ref, key_ref, turned_ref, after_ref,
    oa_ref, ob_ref, la_ref, lb_ref,
):
    requests, _, rows = la_ref.shape
    span = key_ref.shape[1]
    heads = rows // tokens

    position = lax.broadcasted_iota(jnp.int32, (1, span), 1)

    def score(r):
        query = jnp.concatenate(
            [
                jnp.concatenate([qa_ref[first + r], ra_ref[first + r]], axis=1),
                jnp.concatenate([qb_ref[first + r], rb_ref[first + r]], axis=1),
            ],
            axis=0,
        )
        return jnp.dot(query, turned_ref[first + r], preferred_element_type=f32)

    ahead = score(0)
    for r in range(requests):
        scores = ahead * factor
        if r + 1 < requests:
            ahead = score(r + 1)
        limit = length_ref[first + r] - tokens - lax.axis_index("tensor") * span
        bias = [
            jnp.where(position <= limit + t, 0.0, masked_score).astype(f32) for t in range(tokens)
        ]
        scores = jnp.concatenate(
            [scores[k * heads : (k + 1) * heads] + bias[k % tokens] for k in range(2 * tokens)], axis=0
        )
        peak = jnp.max(scores, axis=1, keepdims=True)
        weights = jnp.exp2(scores - peak)
        total = jnp.sum(weights, axis=1, keepdims=True)
        mixture = jnp.dot(weights.astype(bf16), key_ref[first + r], preferred_element_type=f32)
        mixture = (mixture * (1.0 / total)).astype(bf16)
        oa_ref[r] = mixture[:rows]
        ob_ref[r] = mixture[rows:]
        level = jnp.broadcast_to(peak + jnp.log2(total), (2 * rows, 128)).T[:1]
        la_ref[r] = level[:, :rows]
        lb_ref[r] = level[:, rows:]


def attend(first, requests, lengths, qa, qb, ra, rb, key, turned, after, tokens, factor):
    _, rows, width = qa.shape
    span = key.shape[1]
    mixed = jax.ShapeDtypeStruct((requests, rows, width), bf16)
    level = jax.ShapeDtypeStruct((requests, 1, rows), f32)
    return pl.pallas_call(
        functools.partial(attend_kernel, first, tokens, factor),
        in_specs=[SMEM] + [VMEM] * 6 + [pl.BlockSpec(memory_space=pl.ANY)],
        out_specs=[VMEM] * 4,
        out_shape=[mixed, mixed, level, level],
        compiler_params=pltpu.CompilerParams(vmem_limit_bytes=8 << 20),
        cost_estimate=pl.CostEstimate(
            flops=4 * requests * rows * span * (2 * width + 64),
            bytes_accessed=requests * span * width * 2,
            transcendentals=2 * requests * rows * span,
        ),
        name="attend",
    )(lengths, qa, qb, ra, rb, key, turned, after)


def weigh(parts, levels):
    top = functools.reduce(jnp.maximum, levels)
    shares = [jnp.exp2(level - top) for level in levels]
    total = functools.reduce(jnp.add, shares)
    columns = [jnp.swapaxes(share / total, 1, 2) for share in shares]
    joined = functools.reduce(
        jnp.add, [part.astype(f32) * column for part, column in zip(parts, columns)]
    )
    return joined, top + jnp.log2(total)


def local(tensor, q_nope, q_rope, w_uk, w_uv, cache_latent, cache_rope, scale_pool, block_index, lengths):
    requests, tokens, heads, nope_width = q_nope.shape
    rope_width = q_rope.shape[3]
    width = w_uk.shape[2]
    rows = tokens * heads
    chips = tensor // 2
    factor = (nope_width + rope_width) ** -0.5 * math.log2(math.e)
    halves = math.gcd(requests, 2)
    half = requests // halves

    def move(x, chip, core):
        pairs = [(i, 2 * ((i // 2 + chip) % chips) + ((i % 2) ^ core)) for i in range(tensor)]
        return lax.ppermute(x, "tensor", pairs)

    def cross(x):
        return {d: move(x, d, 0) for d in range(1, chips)}

    def spread(x, crossed):
        found = {(0, 0): x, (0, 1): move(x, 0, 1)}
        for d in range(1, chips):
            found[d, 0] = crossed[d]
        for d in range(1, chips):
            found[d, 1] = move(crossed[d], 0, 1)
        return found

    own = (
        jnp.einsum("rthn,hnc->rthc", q_nope, w_uk, preferred_element_type=f32)
        .astype(bf16)
        .reshape(requests, rows, width)
    )
    rope_rows = q_rope.reshape(requests, rows, rope_width)
    own, rope_rows, scale_pool = lax.optimization_barrier((own, rope_rows, scale_pool))
    scales = spread(scale_pool, cross(scale_pool))
    ropes = spread(rope_rows, cross(rope_rows))
    query = spread(own, cross(own))
    table = jnp.stack(list(scales.values()))
    cache = prepare(0, requests, block_index, table, cache_latent, cache_rope)
    after = lengths
    back, own_parts = [], []
    for d in [*range(1, chips), 0]:
        pieces = halves if d == 0 else 1
        count = requests // pieces
        for h in range(pieces):
            oa, ob, la, lb = attend(
                h * count, count, lengths, query[d, 0], query[d, 1], ropes[d, 0], ropes[d, 1], *cache, after, tokens, factor
            )
            after = la
            ob, lb = move(ob, 0, 1), move(lb, 0, 1)
            if d == 0:
                own_parts.append(([oa, ob], [la, lb]))
            else:
                joined, level = weigh([oa, ob], [la, lb])
                level = move(level, -d, 0)
                back.append((move(joined.astype(bf16), -d, 0), level))
    attended = jnp.concatenate(
        [
            weigh(
                parts + [x[h * half : (h + 1) * half] for x, _ in back],
                levels + [y[h * half : (h + 1) * half] for _, y in back],
            )[0].astype(bf16)
            for h, (parts, levels) in enumerate(own_parts)
        ]
    )
    attended = attended.reshape(requests, tokens, heads, width)
    projected = jnp.einsum("rthc,hcv->rthv", attended, w_uv, preferred_element_type=f32)
    return projected.astype(bf16)


def solution(mesh):
    placed = (
        P("dp", None, "tensor", None),
        P("dp", None, "tensor", None),
        P("tensor", None, None),
        P("tensor", None, None),
        P("dp", "tensor", None),
        P("dp", None, "tensor"),
        P(None, ("dp", "tensor")),
        P("dp", "tensor"),
        P("dp"),
    )

    def body(*args):
        return local(mesh.shape["tensor"], *args)

    return jax.shard_map(
        body,
        mesh=mesh,
        in_specs=placed,
        out_specs=P("dp", None, "tensor", None),
        check_vma=False,
    )
```

profile of v0, /device:TPU:0, one launch (start us, length us, event | category | flops | bytes accessed | tf_op | source)
XLA Modules:
  0.0 47.7 jit_solution(16457269625919507783)
XLA Ops:
  0.0 0.0 copy-start
  0.0 0.8 %copy-done = bf16[4,2,32,128]{3,2,1,0:T(8,128)(2,1)S(1)} copy-done((bf16[4,2,32,128]{3,2,1,0:T(8,128)(2,1)S(1)}, bf16[4,2,32,128]{3,2,1,0:T(8,128)(2,1)}, u32[]{:S(2)}) %copy-start) | copy-done | bytes 65560
  0.8 2.8 %fusion.7 = bf16[4,2,32,512]{3,0,1,2:T(4,128)(2,1)S(1)} fusion(bf16[32,128,512]{2,1,0:T(8,128)(2,1)} %param.11, bf16[4,2,32,128]{3,2,1,0:T(8,128)(2,1)S(1)} %copy-done), kind=kOutput, calls=%fused_computation.5 | convolution fusion | flops 33685504 | bytes 4521984 | tf_op jit(solution)/shard_map/rthn,hnc->rthc/dot_general | solution.py:196
  3.7 0.1 copy.11
  3.8 3.0 %collective-permute-start.5 = (bf16[4,64,512]{2,1,0:T(8,128)(2,1)S(1)}, bf16[4,64,512]{2,1,0:T(8,128)(2,1)S(1)}, u32[]{:S(2)}, u32[]{:S(2)}) collective-permute-start(bf16[4,64,512]{2,1,0:T(8,128)(2,1)S(1)} %bitcast.37), channel_id=1, source_target_pairs={{0,2},{1,3},{2,0},{3,1},{4,6},{5,7},{6,4},{7,5},{8,10},{9,11},{10,... | collective-permute-start | bytes 786440 | tf_op jit(solution)/shard_map/ppermute | solution.py:182
  6.8 6.3 %collective-permute-done.5.qa_ref = bf16[4,64,512]{2,1,0:T(8,128)(2,1)S(1)} collective-permute-done((bf16[4,64,512]{2,1,0:T(8,128)(2,1)S(1)}, bf16[4,64,512]{2,1,0:T(8,128)(2,1)S(1)}, u32[]{:S(2)}, u32[]{:S(2)}) %collective-permute-start.5) | collective-permute-done | bytes 262176 | tf_op jit(solution)/shard_map/ppermute | solution.py:182
  13.1 0.0 collective-permute-start.6
  13.1 0.0 copy-done.1
  13.1 1.7 %collective-permute-start.7 = (bf16[4,64,64]{2,1,0:T(8,128)(2,1)S(1)}, bf16[4,64,64]{2,1,0:T(8,128)(2,1)S(1)}, u32[]{:S(2)}, u32[]{:S(2)}) collective-permute-start(bf16[4,64,64]{2,1,0:T(8,128)(2,1)S(1)} %bitcast.41), channel_id=1, source_target_pairs={{0,2},{1,3},{2,0},{3,1},{4,6},{5,7},{6,4},{7,5},{8,10},{9,11},{10,... | collective-permute-start | bytes 98312 | tf_op jit(solution)/shard_map/ppermute | solution.py:182
  14.9 0.3 collective-permute-start.3
  15.1 0.0 collective-permute-start.2
  15.2 3.3 %collective-permute-done.3 = f32[5,64]{1,0:T(8,128)S(1)} collective-permute-done((f32[5,64]{1,0:T(8,128)S(1)}, f32[5,64]{1,0:T(8,128)S(1)}, u32[]{:S(2)}, u32[]{:S(2)}) %collective-permute-start.3) | collective-permute-done | bytes 1312 | tf_op jit(solution)/shard_map/ppermute | solution.py:182
  18.5 0.0 collective-permute-start.4
  18.5 0.5 %collective-permute-start = (bf16[4,64,512]{2,1,0:T(8,128)(2,1)S(1)}, bf16[4,64,512]{2,1,0:T(8,128)(2,1)S(1)}, u32[]{:S(2)}, u32[]{:S(2)}) collective-permute-start(bf16[4,64,512]{2,1,0:T(8,128)(2,1)S(1)} %bitcast.38), channel_id=1, source_target_pairs={{0,1},{1,0},{2,3},{3,2},{4,5},{5,4},{6,7},{7,6},{8,9},{9,8},{10,11... | collective-permute-start | bytes 786440 | tf_op jit(solution)/shard_map/ppermute | solution.py:182
  19.0 0.0 collective-permute-done.2
  19.0 0.0 collective-permute-start.1
  19.0 0.0 collective-permute-done.7.ra_ref
  19.0 0.5 %collective-permute-start.8 = (bf16[4,64,64]{2,1,0:T(8,128)(2,1)S(1)}, bf16[4,64,64]{2,1,0:T(8,128)(2,1)S(1)}, u32[]{:S(2)}, u32[]{:S(2)}) collective-permute-start(bf16[4,64,64]{2,1,0:T(8,128)(2,1)S(1)} %collective-permute-done.7.ra_ref), channel_id=1, source_target_pairs={{0,1},{1,0},{2,3},{3,2},{4,5},{5,4},{6,7},{7,6},{8,9},{9,8},{10,11... | collective-permute-start | bytes 98312 | tf_op jit(solution)/shard_map/ppermute | solution.py:182
  19.5 0.1 collective-permute-done.4
  19.6 0.0 copy-start.2
  19.7 6.0 %prepare.1 = (bf16[4,2048,512]{2,1,0:T(8,128)(2,1)S(1)}, bf16[4,576,2048]{2,1,0:T(8,128)(2,1)S(1)}) custom-call(s32[4,16]{1,0:T(4,128)S(1)} %copy-done.3, f32[4,5,64]{2,1,0:T(8,128)S(1)} %pad_maximum_fusion.1.scale_ref, bf16[4,2048,512]{2,1,0:T(8,128)(2,1)} %latent_hbm.1, bf16[4,64,2048]{2,1,0:T(8,128)(2,1)} %rope_hbm.1), custom_call_target="tpu_custom_call" | custom-call | flops 20000000 | bytes 20000000 | tf_op jit(solution)/shard_map/prepare/pallas_call | solution.py:70
  25.7 0.0 collective-permute-done.8.rb_ref
  25.7 0.0 collective-permute-done.6.qb_ref
  25.7 4.2 %attend.3 = (bf16[4,64,512]{2,1,0:T(8,128)(2,1)S(1)}, bf16[4,64,512]{2,1,0:T(8,128)(2,1)S(1)}, f32[4,1,64]{2,1,0:T(1,128)S(1)}, f32[4,1,64]{2,1,0:T(1,128)S(1)}) custom-call(s32[4]{0:T(128)S(1)} %copy-done.2, bf16[4,64,512]{2,1,0:T(8,128)(2,1)S(1)} %collective-permute-done.5.qa_ref, bf16[4,64,512]{2,1,0:T(8,128)(2,1)S(1)} %collective-permute-done.6.qb_ref, ...), custom_call_target="tpu_custom_call" | custom-call | flops 2281701376 | bytes 8388608 | tf_op jit(solution)/shard_map/attend/pallas_call | solution.py:144
  29.9 0.2 collective-permute-start.10
  30.1 0.0 collective-permute-done.1.rb_ref
  30.1 0.0 collective-permute-done.qb_ref
  30.1 2.3 %attend.4 = (bf16[2,64,512]{2,1,0:T(8,128)(2,1)S(1)}, bf16[2,64,512]{2,1,0:T(8,128)(2,1)S(1)}, f32[2,1,64]{2,1,0:T(1,128)S(1)}, f32[2,1,64]{2,1,0:T(1,128)S(1)}) custom-call(s32[4]{0:T(128)S(1)} %copy-done.2, bf16[4,64,512]{2,1,0:T(8,128)(2,1)S(1)} %bitcast.39, bf16[4,64,512]{2,1,0:T(8,128)(2,1)S(1)} %collective-permute-done.qb_ref, ...), custom_call_target="tpu_custom_call" | custom-call | flops 1140850688 | bytes 4194304 | tf_op jit(solution)/shard_map/attend/pallas_call | solution.py:144
  32.4 0.4 collective-permute-start.9
  32.8 0.2 collective-permute-start.13
  33.0 0.0 collective-permute-done.10
  33.0 1.0 %collective-permute-start.11 = (f32[4,1,64]{2,1,0:T(1,128)S(1)}, f32[4,1,64]{2,1,0:T(1,128)S(1)}, u32[]{:S(2)}, u32[]{:S(2)}) collective-permute-start(f32[4,1,64]{2,1,0:T(1,128)S(1)} %get-tuple-element.49), channel_id=1, source_target_pairs={{0,2},{1,3},{2,0},{3,1},{4,6},{5,7},{6,4},{7,5},{8,10},{9,11},{10,... | collective-permute-start | bytes 3080 | tf_op jit(solution)/shard_map/ppermute | solution.py:182
  34.1 2.3 %attend.5 = (bf16[2,64,512]{2,1,0:T(8,128)(2,1)S(1)}, bf16[2,64,512]{2,1,0:T(8,128)(2,1)S(1)}, f32[2,1,64]{2,1,0:T(1,128)S(1)}, f32[2,1,64]{2,1,0:T(1,128)S(1)}) custom-call(s32[4]{0:T(128)S(1)} %copy-done.2, bf16[4,64,512]{2,1,0:T(8,128)(2,1)S(1)} %bitcast.40, bf16[4,64,512]{2,1,0:T(8,128)(2,1)S(1)} %collective-permute-done.qb_ref, ...), custom_call_target="tpu_custom_call" | custom-call | flops 1140850688 | bytes 4194304 | tf_op jit(solution)/shard_map/attend/pallas_call | solution.py:144
  36.4 0.1 collective-permute-start.16
  36.5 0.5 collective-permute-start.15
  37.0 0.0 collective-permute-done.9
  37.0 0.1 collective-permute-start.12
  37.1 0.0 collective-permute-done.11
  37.1 0.0 collective-permute-done.13
  37.1 0.2 add_convert_fusion
  37.3 1.1 %collective-permute-start.14 = (bf16[4,64,512]{2,1,0:T(8,128)(2,1)S(1)}, bf16[4,64,512]{2,1,0:T(8,128)(2,1)S(1)}, u32[]{:S(2)}, u32[]{:S(2)}) collective-permute-start(bf16[4,64,512]{2,1,0:T(8,128)(2,1)S(1)} %add_convert_fusion), channel_id=1, source_target_pairs={{0,2},{1,3},{2,0},{3,1},{4,6},{5,7},{6,4},{7,5},{8,10},{9,11},{10,... | collective-permute-start | bytes 786440 | tf_op jit(solution)/shard_map/ppermute | solution.py:182
  38.4 0.0 collective-permute-done.15
  38.4 0.0 collective-permute-done.16
  38.4 0.0 collective-permute-done.12
  38.5 7.5 %collective-permute-done.14 = bf16[4,64,512]{2,1,0:T(8,128)(2,1)S(1)} collective-permute-done((bf16[4,64,512]{2,1,0:T(8,128)(2,1)S(1)}, bf16[4,64,512]{2,1,0:T(8,128)(2,1)S(1)}, u32[]{:S(2)}, u32[]{:S(2)}) %collective-permute-start.14) | collective-permute-done | bytes 262176 | tf_op jit(solution)/shard_map/ppermute | solution.py:182
  46.0 0.2 add_convert_fusion.2
  46.3 0.7 %fusion.13 = bf16[4,2,32,128]{3,0,1,2:T(4,128)(2,1)S(1)} fusion(bf16[32,512,128]{2,1,0:T(8,128)(2,1)S(1)} %copy-done.4, bf16[4,2,32,512]{3,2,1,0:T(8,128)(2,1)S(1)} %bitcast.45), kind=kOutput, calls=%fused_computation.7 | convolution fusion | flops 33587200 | bytes 4521984 | tf_op jit(solution)/shard_map/rthc,hcv->rthv/dot_general | solution.py:234
  47.0 0.7 %copy.13 = bf16[4,2,32,128]{3,2,1,0:T(8,128)(2,1)} copy(bf16[4,2,32,128]{3,0,1,2:T(4,128)(2,1)S(1)} %fusion.13) | data formatting | bytes 131072 | tf_op jit(solution)/shard_map/convert_element_type | solution.py:235
  (14 shorter events, 0.1 us)
Async XLA Ops:
  0.0 0.8 %copy-start = (bf16[4,2,32,128]{3,2,1,0:T(8,128)(2,1)S(1)}, bf16[4,2,32,128]{3,2,1,0:T(8,128)(2,1)}, u32[]{:S(2)}) copy-start(bf16[4,2,32,128]{3,2,1,0:T(8,128)(2,1)} %param.9) | copy-start | bytes 196612
  0.0 13.1 %copy-start.1 = (bf16[4,2,32,64]{3,2,1,0:T(8,128)(2,1)S(1)}, bf16[4,2,32,64]{3,2,1,0:T(8,128)(2,1)}, u32[]{:S(2)}) copy-start(bf16[4,2,32,64]{3,2,1,0:T(8,128)(2,1)} %param.10) | copy-start | bytes 98308
  0.0 14.9 %copy-start.5 = (f32[5,64]{1,0:T(8,128)S(1)}, f32[5,64]{1,0:T(8,128)}, u32[]{:S(2)}) copy-start(f32[5,64]{1,0:T(8,128)} %param.15) | copy-start | bytes 3844
  0.0 19.6 %copy-start.3 = (s32[4,16]{1,0:T(4,128)S(1)}, s32[4,16]{1,0:T(4,128)}, u32[]{:S(2)}) copy-start(s32[4,16]{1,0:T(4,128)} %index_ref.1) | copy-start | bytes 772
  3.8 9.3 %collective-permute-start.5 = (bf16[4,64,512]{2,1,0:T(8,128)(2,1)S(1)}, bf16[4,64,512]{2,1,0:T(8,128)(2,1)S(1)}, u32[]{:S(2)}, u32[]{:S(2)}) collective-permute-start(bf16[4,64,512]{2,1,0:T(8,128)(2,1)S(1)} %bitcast.37), channel_id=1, source_target_pairs={{0,2},{1,3},{2,0},{3,1},{4,6},{5,7},{6,4},{7,5},{8,10},{9,11},{10,... | collective-permute-start | bytes 786440 | tf_op jit(solution)/shard_map/ppermute | solution.py:182
  13.1 12.6 %collective-permute-start.6 = (bf16[4,64,512]{2,1,0:T(8,128)(2,1)S(1)}, bf16[4,64,512]{2,1,0:T(8,128)(2,1)S(1)}, u32[]{:S(2)}, u32[]{:S(2)}) collective-permute-start(bf16[4,64,512]{2,1,0:T(8,128)(2,1)S(1)} %collective-permute-done.5.qa_ref), channel_id=1, source_target_pairs={{0,1},{1,0},{2,3},{3,2},{4,5},{5,4},{6,7},{7,6},{8,9},{9,8},{10,11... | collective-permute-start | bytes 786440 | tf_op jit(solution)/shard_map/ppermute | solution.py:182
  13.1 5.9 %collective-permute-start.7 = (bf16[4,64,64]{2,1,0:T(8,128)(2,1)S(1)}, bf16[4,64,64]{2,1,0:T(8,128)(2,1)S(1)}, u32[]{:S(2)}, u32[]{:S(2)}) collective-permute-start(bf16[4,64,64]{2,1,0:T(8,128)(2,1)S(1)} %bitcast.41), channel_id=1, source_target_pairs={{0,2},{1,3},{2,0},{3,1},{4,6},{5,7},{6,4},{7,5},{8,10},{9,11},{10,... | collective-permute-start | bytes 98312 | tf_op jit(solution)/shard_map/ppermute | solution.py:182
  14.9 3.6 %collective-permute-start.3 = (f32[5,64]{1,0:T(8,128)S(1)}, f32[5,64]{1,0:T(8,128)S(1)}, u32[]{:S(2)}, u32[]{:S(2)}) collective-permute-start(f32[5,64]{1,0:T(8,128)S(1)} %copy-done.5), channel_id=1, source_target_pairs={{0,2},{1,3},{2,0},{3,1},{4,6},{5,7},{6,4},{7,5},{8,10},{9,11},{10,... | collective-permute-start | bytes 3848 | tf_op jit(solution)/shard_map/ppermute | solution.py:182
  15.1 3.8 %collective-permute-start.2 = (f32[5,64]{1,0:T(8,128)S(1)}, f32[5,64]{1,0:T(8,128)S(1)}, u32[]{:S(2)}, u32[]{:S(2)}) collective-permute-start(f32[5,64]{1,0:T(8,128)S(1)} %copy-done.5), channel_id=1, source_target_pairs={{0,1},{1,0},{2,3},{3,2},{4,5},{5,4},{6,7},{7,6},{8,9},{9,8},{10,11... | collective-permute-start | bytes 3848 | tf_op jit(solution)/shard_map/ppermute | solution.py:182
  18.5 1.2 %collective-permute-start.4 = (f32[5,64]{1,0:T(8,128)S(1)}, f32[5,64]{1,0:T(8,128)S(1)}, u32[]{:S(2)}, u32[]{:S(2)}) collective-permute-start(f32[5,64]{1,0:T(8,128)S(1)} %collective-permute-done.3), channel_id=1, source_target_pairs={{0,1},{1,0},{2,3},{3,2},{4,5},{5,4},{6,7},{7,6},{8,9},{9,8},{10,11... | collective-permute-start | bytes 3848 | tf_op jit(solution)/shard_map/ppermute | solution.py:182
  18.5 11.6 %collective-permute-start = (bf16[4,64,512]{2,1,0:T(8,128)(2,1)S(1)}, bf16[4,64,512]{2,1,0:T(8,128)(2,1)S(1)}, u32[]{:S(2)}, u32[]{:S(2)}) collective-permute-start(bf16[4,64,512]{2,1,0:T(8,128)(2,1)S(1)} %bitcast.38), channel_id=1, source_target_pairs={{0,1},{1,0},{2,3},{3,2},{4,5},{5,4},{6,7},{7,6},{8,9},{9,8},{10,11... | collective-permute-start | bytes 786440 | tf_op jit(solution)/shard_map/ppermute | solution.py:182
  19.0 11.1 %collective-permute-start.1 = (bf16[4,64,64]{2,1,0:T(8,128)(2,1)S(1)}, bf16[4,64,64]{2,1,0:T(8,128)(2,1)S(1)}, u32[]{:S(2)}, u32[]{:S(2)}) collective-permute-start(bf16[4,64,64]{2,1,0:T(8,128)(2,1)S(1)} %bitcast.42), channel_id=1, source_target_pairs={{0,1},{1,0},{2,3},{3,2},{4,5},{5,4},{6,7},{7,6},{8,9},{9,8},{10,11... | collective-permute-start | bytes 98312 | tf_op jit(solution)/shard_map/ppermute | solution.py:182
  19.0 6.7 %collective-permute-start.8 = (bf16[4,64,64]{2,1,0:T(8,128)(2,1)S(1)}, bf16[4,64,64]{2,1,0:T(8,128)(2,1)S(1)}, u32[]{:S(2)}, u32[]{:S(2)}) collective-permute-start(bf16[4,64,64]{2,1,0:T(8,128)(2,1)S(1)} %collective-permute-done.7.ra_ref), channel_id=1, source_target_pairs={{0,1},{1,0},{2,3},{3,2},{4,5},{5,4},{6,7},{7,6},{8,9},{9,8},{10,11... | collective-permute-start | bytes 98312 | tf_op jit(solution)/shard_map/ppermute | solution.py:182
  19.6 6.0 %copy-start.2 = (s32[4]{0:T(128)S(1)}, s32[4]{0:T(128)}, u32[]{:S(2)}) copy-start(s32[4]{0:T(128)} %length_ref.5) | copy-start | bytes 52
  29.9 3.1 %collective-permute-start.10 = (f32[4,1,64]{2,1,0:T(1,128)S(1)}, f32[4,1,64]{2,1,0:T(1,128)S(1)}, u32[]{:S(2)}, u32[]{:S(2)}) collective-permute-start(f32[4,1,64]{2,1,0:T(1,128)S(1)} %get-tuple-element.31), channel_id=1, source_target_pairs={{0,1},{1,0},{2,3},{3,2},{4,5},{5,4},{6,7},{7,6},{8,9},{9,8},{10,11... | collective-permute-start | bytes 3080 | tf_op jit(solution)/shard_map/ppermute | solution.py:182
  32.4 4.6 %collective-permute-start.9 = (f32[2,1,64]{2,1,0:T(1,128)S(1)}, f32[2,1,64]{2,1,0:T(1,128)S(1)}, u32[]{:S(2)}, u32[]{:S(2)}) collective-permute-start(f32[2,1,64]{2,1,0:T(1,128)S(1)} %get-tuple-element.30), channel_id=1, source_target_pairs={{0,1},{1,0},{2,3},{3,2},{4,5},{5,4},{6,7},{7,6},{8,9},{9,8},{10,11... | collective-permute-start | bytes 1544 | tf_op jit(solution)/shard_map/ppermute | solution.py:182
  32.8 4.2 %collective-permute-start.13 = (bf16[4,64,512]{2,1,0:T(8,128)(2,1)S(1)}, bf16[4,64,512]{2,1,0:T(8,128)(2,1)S(1)}, u32[]{:S(2)}, u32[]{:S(2)}) collective-permute-start(bf16[4,64,512]{2,1,0:T(8,128)(2,1)S(1)} %get-tuple-element.34), channel_id=1, source_target_pairs={{0,1},{1,0},{2,3},{3,2},{4,5},{5,4},{6,7},{7,6},{8,9},{9,8},{10,11... | collective-permute-start | bytes 786440 | tf_op jit(solution)/shard_map/ppermute | solution.py:182
  33.0 4.0 %collective-permute-start.11 = (f32[4,1,64]{2,1,0:T(1,128)S(1)}, f32[4,1,64]{2,1,0:T(1,128)S(1)}, u32[]{:S(2)}, u32[]{:S(2)}) collective-permute-start(f32[4,1,64]{2,1,0:T(1,128)S(1)} %get-tuple-element.49), channel_id=1, source_target_pairs={{0,2},{1,3},{2,0},{3,1},{4,6},{5,7},{6,4},{7,5},{8,10},{9,11},{10,... | collective-permute-start | bytes 3080 | tf_op jit(solution)/shard_map/ppermute | solution.py:182
  34.1 12.2 %copy-start.4 = (bf16[32,512,128]{2,1,0:T(8,128)(2,1)S(1)}, bf16[32,512,128]{2,1,0:T(8,128)(2,1)}, u32[]{:S(2)}) copy-start(bf16[32,512,128]{2,1,0:T(8,128)(2,1)} %param.12) | copy-start | bytes 12582916
  36.4 2.0 %collective-permute-start.16 = (bf16[2,64,512]{2,1,0:T(8,128)(2,1)S(1)}, bf16[2,64,512]{2,1,0:T(8,128)(2,1)S(1)}, u32[]{:S(2)}, u32[]{:S(2)}) collective-permute-start(bf16[2,64,512]{2,1,0:T(8,128)(2,1)S(1)} %get-tuple-element.38), channel_id=1, source_target_pairs={{0,1},{1,0},{2,3},{3,2},{4,5},{5,4},{6,7},{7,6},{8,9},{9,8},{10,11... | collective-permute-start | bytes 393224 | tf_op jit(solution)/shard_map/ppermute | solution.py:182
  36.5 1.9 %collective-permute-start.15 = (f32[2,1,64]{2,1,0:T(1,128)S(1)}, f32[2,1,64]{2,1,0:T(1,128)S(1)}, u32[]{:S(2)}, u32[]{:S(2)}) collective-permute-start(f32[2,1,64]{2,1,0:T(1,128)S(1)} %get-tuple-element.37), channel_id=1, source_target_pairs={{0,1},{1,0},{2,3},{3,2},{4,5},{5,4},{6,7},{7,6},{8,9},{9,8},{10,11... | collective-permute-start | bytes 1544 | tf_op jit(solution)/shard_map/ppermute | solution.py:182
  37.0 1.5 %collective-permute-start.12 = (bf16[2,64,512]{2,1,0:T(8,128)(2,1)S(1)}, bf16[2,64,512]{2,1,0:T(8,128)(2,1)S(1)}, u32[]{:S(2)}, u32[]{:S(2)}) collective-permute-start(bf16[2,64,512]{2,1,0:T(8,128)(2,1)S(1)} %get-tuple-element.32), channel_id=1, source_target_pairs={{0,1},{1,0},{2,3},{3,2},{4,5},{5,4},{6,7},{7,6},{8,9},{9,8},{10,11... | collective-permute-start | bytes 393224 | tf_op jit(solution)/shard_map/ppermute | solution.py:182
  37.3 8.7 %collective-permute-start.14 = (bf16[4,64,512]{2,1,0:T(8,128)(2,1)S(1)}, bf16[4,64,512]{2,1,0:T(8,128)(2,1)S(1)}, u32[]{:S(2)}, u32[]{:S(2)}) collective-permute-start(bf16[4,64,512]{2,1,0:T(8,128)(2,1)S(1)} %add_convert_fusion), channel_id=1, source_target_pairs={{0,2},{1,3},{2,0},{3,1},{4,6},{5,7},{6,4},{7,5},{8,10},{9,11},{10,... | collective-permute-start | bytes 786440 | tf_op jit(solution)/shard_map/ppermute | solution.py:182
where the time goes:
time: 47.9 us; the launch traced here: 47.7 us
  waiting for transfers between devices  17.3 us (36%)
  Pallas kernels  14.9 us (31%)
  starting transfers between devices  9.64 us (20%)
  matrix products  3.57 us (7%)
  local copies, waits for them, and re-layouts  1.59 us (3%)
  other arithmetic  0.53 us (1%)
    ppermute x17, waiting for transfers between devices, move(): return lax.ppermute(x, 'tensor', pairs)  17.3 us
    ppermute x17, starting transfers between devices, move(): return lax.ppermute(x, 'tensor', pairs)  9.64 us
    pallas_call x3, Pallas kernels, attend(): pl.pallas_call(functools.partial(attend_kernel, first, tokens, factor), i...  8.85 us
    pallas_call x1, Pallas kernels, prepare(): pl.pallas_call(functools.partial(prepare_kernel, first, pieces), in_specs...  6 us
    dot_general x1, matrix products, local(): jnp.einsum('rthn,hnc->rthc', q_nope, w_uk, preferred_element_type=f32)  2.84 us
  transfers between devices with their start and end apart: 17, of which 4 were waited for; matrix products, arithmetic and copies ran while one was open for 1% of the time, Pallas kernels for 31%

commit v1 on v0

--- a/solution.py
+++ b/solution.py
@@ -105,8 +105,8 @@
     def score(r):
         query = jnp.concatenate(
             [
-                jnp.concatenate([qa_ref[first + r], ra_ref[first + r]], axis=1),
-                jnp.concatenate([qb_ref[first + r], rb_ref[first + r]], axis=1),
+                jnp.concatenate([qa_ref[r], ra_ref[first + r]], axis=1),
+                jnp.concatenate([qb_ref[r], rb_ref[first + r]], axis=1),
             ],
             axis=0,
         )
@@ -136,8 +136,8 @@
         lb_ref[r] = level[:, rows:]
 
 
-def attend(first, requests, lengths, qa, qb, ra, rb, key, turned, after, tokens, factor):
-    _, rows, width = qa.shape
+def attend(first, lengths, qa, qb, ra, rb, key, turned, after, tokens, factor):
+    requests, rows, width = qa.shape
     span = key.shape[1]
     mixed = jax.ShapeDtypeStruct((requests, rows, width), bf16)
     level = jax.ShapeDtypeStruct((requests, 1, rows), f32)
@@ -173,9 +173,8 @@
     width = w_uk.shape[2]
     rows = tokens * heads
     chips = tensor // 2
+    half = requests // 2 if chips == 2 and requests % 2 == 0 else requests
     factor = (nope_width + rope_width) ** -0.5 * math.log2(math.e)
-    halves = math.gcd(requests, 2)
-    half = requests // halves
 
     def move(x, chip, core):
         pairs = [(i, 2 * ((i // 2 + chip) % chips) + ((i % 2) ^ core)) for i in range(tensor)]
@@ -198,38 +197,38 @@
         .reshape(requests, rows, width)
     )
     rope_rows = q_rope.reshape(requests, rows, rope_width)
-    own, rope_rows, scale_pool = lax.optimization_barrier((own, rope_rows, scale_pool))
     scales = spread(scale_pool, cross(scale_pool))
     ropes = spread(rope_rows, cross(rope_rows))
-    query = spread(own, cross(own))
+    halves = [own[h * half : (h + 1) * half] for h in range(requests // half)]
+    crossed = [cross(x) for x in halves]
+    query = [{(d, 0): crossed[h][d] for d in range(1, chips)} for h in range(len(halves))]
+    for h in range(len(halves)):
+        for d in range(1, chips):
+            query[h][d, 1] = move(crossed[h][d], 0, 1)
+    partner = move(own, 0, 1)
     table = jnp.stack(list(scales.values()))
     cache = prepare(0, requests, block_index, table, cache_latent, cache_rope)
     after = lengths
-    back, own_parts = [], []
-    for d in [*range(1, chips), 0]:
-        pieces = halves if d == 0 else 1
-        count = requests // pieces
-        for h in range(pieces):
+    parts, levels = [], []
+    for d in range(1, chips):
+        joined, level = [], []
+        for h in range(len(halves)):
             oa, ob, la, lb = attend(
-                h * count, count, lengths, query[d, 0], query[d, 1], ropes[d, 0], ropes[d, 1], *cache, after, tokens, factor
+                h * half, lengths, query[h][d, 0], query[h][d, 1], ropes[d, 0], ropes[d, 1], *cache, after, tokens, factor
             )
             after = la
             ob, lb = move(ob, 0, 1), move(lb, 0, 1)
-            if d == 0:
-                own_parts.append(([oa, ob], [la, lb]))
-            else:
-                joined, level = weigh([oa, ob], [la, lb])
-                level = move(level, -d, 0)
-                back.append((move(joined.astype(bf16), -d, 0), level))
-    attended = jnp.concatenate(
-        [
-            weigh(
-                parts + [x[h * half : (h + 1) * half] for x, _ in back],
-                levels + [y[h * half : (h + 1) * half] for _, y in back],
-            )[0].astype(bf16)
-            for h, (parts, levels) in enumerate(own_parts)
-        ]
-    )
+            both = weigh([oa, ob], [la, lb])
+            joined.append(both[0].astype(bf16))
+            level.append(both[1])
+        levels.append(move(jnp.concatenate(level), -d, 0))
+        parts.append(move(jnp.concatenate(joined), -d, 0))
+    oa, ob, la, lb = attend(
+        0, lengths, own, partner, ropes[0, 0], ropes[0, 1], *cache, after, tokens, factor
+    )
+    parts += [oa, move(ob, 0, 1)]
+    levels += [la, move(lb, 0, 1)]
+    attended = weigh(parts, levels)[0].astype(bf16)
     attended = attended.reshape(requests, tokens, heads, width)
     projected = jnp.einsum("rthc,hcv->rthv", attended, w_uv, preferred_element_type=f32)
     return projected.astype(bf16)

time: 47.9 us -> 45.7 us (0.954)
  waiting for transfers between devices: 17.3 us -> 11.7 us
  starting transfers between devices: 9.64 us -> 13 us
    ppermute x17 -> x19, waiting for transfers between devices: 17.3 us -> 11.7 us  [move(): return lax.ppermute(x, 'tensor', pairs)]
    ppermute x17 -> x19, starting transfers between devices: 9.64 us -> 13 us  [move(): return lax.ppermute(x, 'tensor', pairs)]
  transfers between devices with their start and end apart: 17 -> 19, of which waited for: 4 -> 5; matrix products, arithmetic and copies ran while one was open for 1% -> 1% of each run, Pallas kernels for 31% -> 32%
where the time goes in v1:
time: 45.7 us; the launch traced here: 45.5 us
  Pallas kernels  14.6 us (32%)
  starting transfers between devices  13 us (28%)
  waiting for transfers between devices  11.7 us (26%)
  matrix products  3.59 us (8%)
  local copies, waits for them, and re-layouts  1.82 us (4%)
  other arithmetic  0.6 us (1%)
    ppermute x19, starting transfers between devices, move(): return lax.ppermute(x, 'tensor', pairs)  13 us
    ppermute x19, waiting for transfers between devices, move(): return lax.ppermute(x, 'tensor', pairs)  11.7 us
    pallas_call x3, Pallas kernels, attend(): pl.pallas_call(functools.partial(attend_kernel, first, tokens, factor), i...  8.57 us
    pallas_call x1, Pallas kernels, prepare(): pl.pallas_call(functools.partial(prepare_kernel, first, pieces), in_specs...  5.98 us
    dot_general x1, matrix products, local(): jnp.einsum('rthn,hnc->rthc', q_nope, w_uk, preferred_element_type=f32)  2.84 us
  transfers between devices with their start and end apart: 19, of which 5 were waited for; matrix products, arithmetic and copies ran while one was open for 1% of the time, Pallas kernels for 32%

profile of v1, /device:TPU:0, one launch (start us, length us, event | category | flops | bytes accessed | tf_op | source)
XLA Modules:
  0.0 45.5 jit_solution(6266887939160458423)
XLA Ops:
  0.0 0.8 %copy-done = bf16[4,2,32,128]{3,2,1,0:T(8,128)(2,1)S(1)} copy-done((bf16[4,2,32,128]{3,2,1,0:T(8,128)(2,1)S(1)}, bf16[4,2,32,128]{3,2,1,0:T(8,128)(2,1)}, u32[]{:S(2)}) %copy-start) | copy-done | bytes 65560
  0.8 2.8 %fusion.7 = bf16[4,2,32,512]{3,0,1,2:T(4,128)(2,1)S(1)} fusion(bf16[32,128,512]{2,1,0:T(8,128)(2,1)} %param.11, bf16[4,2,32,128]{3,2,1,0:T(8,128)(2,1)S(1)} %copy-done), kind=kOutput, calls=%fused_computation.5 | convolution fusion | flops 33685504 | bytes 4521984 | tf_op jit(solution)/shard_map/rthn,hnc->rthc/dot_general | solution.py:195
  3.7 0.2 fusion.21
  3.9 3.0 %collective-permute-start = (bf16[2,64,512]{2,1,0:T(8,128)(2,1)S(1)}, bf16[2,64,512]{2,1,0:T(8,128)(2,1)S(1)}, u32[]{:S(2)}, u32[]{:S(2)}) collective-permute-start(bf16[2,64,512]{2,1,0:T(8,128)(2,1)S(1)} %bitcast.45), channel_id=1, source_target_pairs={{0,2},{1,3},{2,0},{3,1},{4,6},{5,7},{6,4},{7,5},{8,10},{9,11},{10,... | collective-permute-start | bytes 393224 | tf_op jit(solution)/shard_map/ppermute | solution.py:181
  7.0 0.1 collective-permute-start.9
  7.1 2.0 %collective-permute-start.2 = (bf16[4,64,64]{2,1,0:T(8,128)(2,1)S(1)}, bf16[4,64,64]{2,1,0:T(8,128)(2,1)S(1)}, u32[]{:S(2)}, u32[]{:S(2)}) collective-permute-start(bf16[4,64,64]{2,1,0:T(8,128)(2,1)S(1)} %bitcast.40), channel_id=1, source_target_pairs={{0,2},{1,3},{2,0},{3,1},{4,6},{5,7},{6,4},{7,5},{8,10},{9,11},{10,... | collective-permute-start | bytes 98312 | tf_op jit(solution)/shard_map/ppermute | solution.py:181
  9.1 2.2 %collective-permute-done.qa_ref = bf16[2,64,512]{2,1,0:T(8,128)(2,1)S(1)} collective-permute-done((bf16[2,64,512]{2,1,0:T(8,128)(2,1)S(1)}, bf16[2,64,512]{2,1,0:T(8,128)(2,1)S(1)}, u32[]{:S(2)}, u32[]{:S(2)}) %collective-permute-start) | collective-permute-done | bytes 131104 | tf_op jit(solution)/shard_map/ppermute | solution.py:181
  11.3 0.0 collective-permute-start.1
  11.3 2.0 %collective-permute-start.5 = (f32[5,64]{1,0:T(8,128)S(1)}, f32[5,64]{1,0:T(8,128)S(1)}, u32[]{:S(2)}, u32[]{:S(2)}) collective-permute-start(f32[5,64]{1,0:T(8,128)S(1)} %copy-done.5), channel_id=1, source_target_pairs={{0,2},{1,3},{2,0},{3,1},{4,6},{5,7},{6,4},{7,5},{8,10},{9,11},{10,... | collective-permute-start | bytes 3848 | tf_op jit(solution)/shard_map/ppermute | solution.py:181
  13.3 0.2 collective-permute-start.4
  13.5 1.4 %collective-permute-done.5 = f32[5,64]{1,0:T(8,128)S(1)} collective-permute-done((f32[5,64]{1,0:T(8,128)S(1)}, f32[5,64]{1,0:T(8,128)S(1)}, u32[]{:S(2)}, u32[]{:S(2)}) %collective-permute-start.5) | collective-permute-done | bytes 1312 | tf_op jit(solution)/shard_map/ppermute | solution.py:181
  14.9 0.0 collective-permute-start.6
  14.9 0.1 copy.13
  15.0 0.0 collective-permute-done.4
  15.0 0.6 %collective-permute-start.16 = (bf16[4,64,64]{2,1,0:T(8,128)(2,1)S(1)}, bf16[4,64,64]{2,1,0:T(8,128)(2,1)S(1)}, u32[]{:S(2)}, u32[]{:S(2)}) collective-permute-start(bf16[4,64,64]{2,1,0:T(8,128)(2,1)S(1)} %bitcast.41), channel_id=1, source_target_pairs={{0,1},{1,0},{2,3},{3,2},{4,5},{5,4},{6,7},{7,6},{8,9},{9,8},{10,11... | collective-permute-start | bytes 98312 | tf_op jit(solution)/shard_map/ppermute | solution.py:181
  15.6 0.5 %collective-permute-done.6 = f32[5,64]{1,0:T(8,128)S(1)} collective-permute-done((f32[5,64]{1,0:T(8,128)S(1)}, f32[5,64]{1,0:T(8,128)S(1)}, u32[]{:S(2)}, u32[]{:S(2)}) %collective-permute-start.6) | collective-permute-done | bytes 1312 | tf_op jit(solution)/shard_map/ppermute | solution.py:181
  16.1 0.2 collective-permute-start.15
  16.2 0.0 collective-permute-done.2.ra_ref
  16.2 0.3 collective-permute-start.3
  16.6 0.0 collective-permute-done.9.qa_ref
  16.6 0.2 collective-permute-start.10
  16.8 0.0 copy-start.2
  16.8 6.0 %prepare.1 = (bf16[4,2048,512]{2,1,0:T(8,128)(2,1)S(1)}, bf16[4,576,2048]{2,1,0:T(8,128)(2,1)S(1)}) custom-call(s32[4,16]{1,0:T(4,128)S(1)} %copy-done.3, f32[4,5,64]{2,1,0:T(8,128)S(1)} %pad_maximum_fusion.1.scale_ref, bf16[4,2048,512]{2,1,0:T(8,128)(2,1)} %latent_hbm.1, bf16[4,64,2048]{2,1,0:T(8,128)(2,1)} %rope_hbm.1), custom_call_target="tpu_custom_call" | custom-call | flops 20000000 | bytes 20000000 | tf_op jit(solution)/shard_map/prepare/pallas_call | solution.py:70
  22.8 0.0 collective-permute-done.3.rb_ref
  22.8 0.0 collective-permute-done.1.qb_ref
  22.8 2.3 %attend.3 = (bf16[2,64,512]{2,1,0:T(8,128)(2,1)S(1)}, bf16[2,64,512]{2,1,0:T(8,128)(2,1)S(1)}, f32[2,1,64]{2,1,0:T(1,128)S(1)}, f32[2,1,64]{2,1,0:T(1,128)S(1)}) custom-call(s32[4]{0:T(128)S(1)} %copy-done.2, bf16[2,64,512]{2,1,0:T(8,128)(2,1)S(1)} %collective-permute-done.qa_ref, bf16[2,64,512]{2,1,0:T(8,128)(2,1)S(1)} %collective-permute-done.1.qb_ref, ...), custom_call_target="tpu_custom_call" | custom-call | flops 1140850688 | bytes 4194304 | tf_op jit(solution)/shard_map/attend/pallas_call | solution.py:144
  25.1 0.4 collective-permute-start.7
  25.5 0.0 collective-permute-done.10.qb_ref
  25.5 2.2 %attend.4 = (bf16[2,64,512]{2,1,0:T(8,128)(2,1)S(1)}, bf16[2,64,512]{2,1,0:T(8,128)(2,1)S(1)}, f32[2,1,64]{2,1,0:T(1,128)S(1)}, f32[2,1,64]{2,1,0:T(1,128)S(1)}) custom-call(s32[4]{0:T(128)S(1)} %copy-done.2, bf16[2,64,512]{2,1,0:T(8,128)(2,1)S(1)} %collective-permute-done.9.qa_ref, bf16[2,64,512]{2,1,0:T(8,128)(2,1)S(1)} %collective-permute-done.10.qb_ref, ...), custom_call_target="tpu_custom_call" | custom-call | flops 1140850688 | bytes 4194304 | tf_op jit(solution)/shard_map/attend/pallas_call | solution.py:144
  27.7 0.2 collective-permute-start.11
  28.0 0.0 collective-permute-done.16.rb_ref
  28.0 0.0 collective-permute-done.15.qb_ref
  28.0 4.1 %attend.5 = (bf16[4,64,512]{2,1,0:T(8,128)(2,1)S(1)}, bf16[4,64,512]{2,1,0:T(8,128)(2,1)S(1)}, f32[4,1,64]{2,1,0:T(1,128)S(1)}, f32[4,1,64]{2,1,0:T(1,128)S(1)}) custom-call(s32[4]{0:T(128)S(1)} %copy-done.2, bf16[4,64,512]{2,1,0:T(8,128)(2,1)S(1)} %bitcast.39, bf16[4,64,512]{2,1,0:T(8,128)(2,1)S(1)} %collective-permute-done.15.qb_ref, ...), custom_call_target="tpu_custom_call" | custom-call | flops 2281701376 | bytes 8388608 | tf_op jit(solution)/shard_map/attend/pallas_call | solution.py:144
  32.0 0.3 collective-permute-start.17
  32.4 0.2 collective-permute-start.8
  32.6 0.3 collective-permute-start.12
  32.9 0.2 collective-permute-start.18
  33.1 0.0 collective-permute-done.11
  33.1 2.1 %collective-permute-start.14 = (f32[4,1,64]{2,1,0:T(1,128)S(1)}, f32[4,1,64]{2,1,0:T(1,128)S(1)}, u32[]{:S(2)}, u32[]{:S(2)}) collective-permute-start(f32[4,1,64]{2,1,0:T(1,128)S(1)} %pad_maximum_fusion.2), channel_id=1, source_target_pairs={{0,2},{1,3},{2,0},{3,1},{4,6},{5,7},{6,4},{7,5},{8,10},{9,11},{10,... | collective-permute-start | bytes 3080 | tf_op jit(solution)/shard_map/ppermute | solution.py:181
  35.2 0.0 collective-permute-done.8
  35.2 0.1 add_convert_fusion.2
  35.4 0.1 add_convert_fusion.1
  35.5 0.6 %collective-permute-start.13 = (bf16[4,64,512]{2,1,0:T(8,128)(2,1)S(1)}, bf16[4,64,512]{2,1,0:T(8,128)(2,1)S(1)}, u32[]{:S(2)}, u32[]{:S(2)}) collective-permute-start(bf16[4,64,512]{2,1,0:T(8,128)(2,1)S(1)} %pad_maximum_fusion), channel_id=1, source_target_pairs={{0,2},{1,3},{2,0},{3,1},{4,6},{5,7},{6,4},{7,5},{8,10},{9,11},{10,... | collective-permute-start | bytes 786440 | tf_op jit(solution)/shard_map/ppermute | solution.py:181
  36.2 0.6 %collective-permute-done.14 = f32[4,1,64]{2,1,0:T(1,128)S(1)} collective-permute-done((f32[4,1,64]{2,1,0:T(1,128)S(1)}, f32[4,1,64]{2,1,0:T(1,128)S(1)}, u32[]{:S(2)}, u32[]{:S(2)}) %collective-permute-start.14) | collective-permute-done | bytes 1056 | tf_op jit(solution)/shard_map/ppermute | solution.py:181
  36.9 7.0 %collective-permute-done.13 = bf16[4,64,512]{2,1,0:T(8,128)(2,1)S(1)} collective-permute-done((bf16[4,64,512]{2,1,0:T(8,128)(2,1)S(1)}, bf16[4,64,512]{2,1,0:T(8,128)(2,1)S(1)}, u32[]{:S(2)}, u32[]{:S(2)}) %collective-permute-start.13) | collective-permute-done | bytes 262176 | tf_op jit(solution)/shard_map/ppermute | solution.py:181
  43.9 0.2 add_convert_fusion
  44.1 0.8 %fusion.13 = bf16[4,2,32,128]{3,0,1,2:T(4,128)(2,1)S(1)} fusion(bf16[32,512,128]{2,1,0:T(8,128)(2,1)S(1)} %copy-done.4, bf16[4,2,32,512]{3,2,1,0:T(8,128)(2,1)S(1)} %bitcast.43), kind=kOutput, calls=%fused_computation.7 | convolution fusion | flops 33587200 | bytes 4521984 | tf_op jit(solution)/shard_map/rthc,hcv->rthv/dot_general | solution.py:233
  44.9 0.7 %copy.15 = bf16[4,2,32,128]{3,2,1,0:T(8,128)(2,1)} copy(bf16[4,2,32,128]{3,0,1,2:T(4,128)(2,1)S(1)} %fusion.13) | data formatting | bytes 131072 | tf_op jit(solution)/shard_map/convert_element_type | solution.py:234
  (23 shorter events, 0.2 us)
Async XLA Ops:
  0.0 0.8 %copy-start = (bf16[4,2,32,128]{3,2,1,0:T(8,128)(2,1)S(1)}, bf16[4,2,32,128]{3,2,1,0:T(8,128)(2,1)}, u32[]{:S(2)}) copy-start(bf16[4,2,32,128]{3,2,1,0:T(8,128)(2,1)} %param.9) | copy-start | bytes 196612
  0.0 7.1 %copy-start.1 = (bf16[4,2,32,64]{3,2,1,0:T(8,128)(2,1)S(1)}, bf16[4,2,32,64]{3,2,1,0:T(8,128)(2,1)}, u32[]{:S(2)}) copy-start(bf16[4,2,32,64]{3,2,1,0:T(8,128)(2,1)} %param.10) | copy-start | bytes 98308
  0.0 11.3 %copy-start.5 = (f32[5,64]{1,0:T(8,128)S(1)}, f32[5,64]{1,0:T(8,128)}, u32[]{:S(2)}) copy-start(f32[5,64]{1,0:T(8,128)} %param.15) | copy-start | bytes 3844
  0.0 16.8 %copy-start.3 = (s32[4,16]{1,0:T(4,128)S(1)}, s32[4,16]{1,0:T(4,128)}, u32[]{:S(2)}) copy-start(s32[4,16]{1,0:T(4,128)} %index_ref.1) | copy-start | bytes 772
  3.9 7.4 %collective-permute-start = (bf16[2,64,512]{2,1,0:T(8,128)(2,1)S(1)}, bf16[2,64,512]{2,1,0:T(8,128)(2,1)S(1)}, u32[]{:S(2)}, u32[]{:S(2)}) collective-permute-start(bf16[2,64,512]{2,1,0:T(8,128)(2,1)S(1)} %bitcast.45), channel_id=1, source_target_pairs={{0,2},{1,3},{2,0},{3,1},{4,6},{5,7},{6,4},{7,5},{8,10},{9,11},{10,... | collective-permute-start | bytes 393224 | tf_op jit(solution)/shard_map/ppermute | solution.py:181
  7.0 9.6 %collective-permute-start.9 = (bf16[2,64,512]{2,1,0:T(8,128)(2,1)S(1)}, bf16[2,64,512]{2,1,0:T(8,128)(2,1)S(1)}, u32[]{:S(2)}, u32[]{:S(2)}) collective-permute-start(bf16[2,64,512]{2,1,0:T(8,128)(2,1)S(1)} %bitcast.44), channel_id=1, source_target_pairs={{0,2},{1,3},{2,0},{3,1},{4,6},{5,7},{6,4},{7,5},{8,10},{9,11},{10,... | collective-permute-start | bytes 393224 | tf_op jit(solution)/shard_map/ppermute | solution.py:181
  7.1 9.2 %collective-permute-start.2 = (bf16[4,64,64]{2,1,0:T(8,128)(2,1)S(1)}, bf16[4,64,64]{2,1,0:T(8,128)(2,1)S(1)}, u32[]{:S(2)}, u32[]{:S(2)}) collective-permute-start(bf16[4,64,64]{2,1,0:T(8,128)(2,1)S(1)} %bitcast.40), channel_id=1, source_target_pairs={{0,2},{1,3},{2,0},{3,1},{4,6},{5,7},{6,4},{7,5},{8,10},{9,11},{10,... | collective-permute-start | bytes 98312 | tf_op jit(solution)/shard_map/ppermute | solution.py:181
  11.3 11.5 %collective-permute-start.1 = (bf16[2,64,512]{2,1,0:T(8,128)(2,1)S(1)}, bf16[2,64,512]{2,1,0:T(8,128)(2,1)S(1)}, u32[]{:S(2)}, u32[]{:S(2)}) collective-permute-start(bf16[2,64,512]{2,1,0:T(8,128)(2,1)S(1)} %collective-permute-done.qa_ref), channel_id=1, source_target_pairs={{0,1},{1,0},{2,3},{3,2},{4,5},{5,4},{6,7},{7,6},{8,9},{9,8},{10,11... | collective-permute-start | bytes 393224 | tf_op jit(solution)/shard_map/ppermute | solution.py:181
  11.3 3.6 %collective-permute-start.5 = (f32[5,64]{1,0:T(8,128)S(1)}, f32[5,64]{1,0:T(8,128)S(1)}, u32[]{:S(2)}, u32[]{:S(2)}) collective-permute-start(f32[5,64]{1,0:T(8,128)S(1)} %copy-done.5), channel_id=1, source_target_pairs={{0,2},{1,3},{2,0},{3,1},{4,6},{5,7},{6,4},{7,5},{8,10},{9,11},{10,... | collective-permute-start | bytes 3848 | tf_op jit(solution)/shard_map/ppermute | solution.py:181
  13.3 1.7 %collective-permute-start.4 = (f32[5,64]{1,0:T(8,128)S(1)}, f32[5,64]{1,0:T(8,128)S(1)}, u32[]{:S(2)}, u32[]{:S(2)}) collective-permute-start(f32[5,64]{1,0:T(8,128)S(1)} %copy-done.5), channel_id=1, source_target_pairs={{0,1},{1,0},{2,3},{3,2},{4,5},{5,4},{6,7},{7,6},{8,9},{9,8},{10,11... | collective-permute-start | bytes 3848 | tf_op jit(solution)/shard_map/ppermute | solution.py:181
  14.9 1.2 %collective-permute-start.6 = (f32[5,64]{1,0:T(8,128)S(1)}, f32[5,64]{1,0:T(8,128)S(1)}, u32[]{:S(2)}, u32[]{:S(2)}) collective-permute-start(f32[5,64]{1,0:T(8,128)S(1)} %collective-permute-done.5), channel_id=1, source_target_pairs={{0,1},{1,0},{2,3},{3,2},{4,5},{5,4},{6,7},{7,6},{8,9},{9,8},{10,11... | collective-permute-start | bytes 3848 | tf_op jit(solution)/shard_map/ppermute | solution.py:181
  15.0 13.0 %collective-permute-start.16 = (bf16[4,64,64]{2,1,0:T(8,128)(2,1)S(1)}, bf16[4,64,64]{2,1,0:T(8,128)(2,1)S(1)}, u32[]{:S(2)}, u32[]{:S(2)}) collective-permute-start(bf16[4,64,64]{2,1,0:T(8,128)(2,1)S(1)} %bitcast.41), channel_id=1, source_target_pairs={{0,1},{1,0},{2,3},{3,2},{4,5},{5,4},{6,7},{7,6},{8,9},{9,8},{10,11... | collective-permute-start | bytes 98312 | tf_op jit(solution)/shard_map/ppermute | solution.py:181
  16.1 11.9 %collective-permute-start.15 = (bf16[4,64,512]{2,1,0:T(8,128)(2,1)S(1)}, bf16[4,64,512]{2,1,0:T(8,128)(2,1)S(1)}, u32[]{:S(2)}, u32[]{:S(2)}) collective-permute-start(bf16[4,64,512]{2,1,0:T(8,128)(2,1)S(1)} %bitcast.38), channel_id=1, source_target_pairs={{0,1},{1,0},{2,3},{3,2},{4,5},{5,4},{6,7},{7,6},{8,9},{9,8},{10,11... | collective-permute-start | bytes 786440 | tf_op jit(solution)/shard_map/ppermute | solution.py:181
  16.2 6.5 %collective-permute-start.3 = (bf16[4,64,64]{2,1,0:T(8,128)(2,1)S(1)}, bf16[4,64,64]{2,1,0:T(8,128)(2,1)S(1)}, u32[]{:S(2)}, u32[]{:S(2)}) collective-permute-start(bf16[4,64,64]{2,1,0:T(8,128)(2,1)S(1)} %collective-permute-done.2.ra_ref), channel_id=1, source_target_pairs={{0,1},{1,0},{2,3},{3,2},{4,5},{5,4},{6,7},{7,6},{8,9},{9,8},{10,11... | collective-permute-start | bytes 98312 | tf_op jit(solution)/shard_map/ppermute | solution.py:181
  16.6 8.9 %collective-permute-start.10 = (bf16[2,64,512]{2,1,0:T(8,128)(2,1)S(1)}, bf16[2,64,512]{2,1,0:T(8,128)(2,1)S(1)}, u32[]{:S(2)}, u32[]{:S(2)}) collective-permute-start(bf16[2,64,512]{2,1,0:T(8,128)(2,1)S(1)} %collective-permute-done.9.qa_ref), channel_id=1, source_target_pairs={{0,1},{1,0},{2,3},{3,2},{4,5},{5,4},{6,7},{7,6},{8,9},{9,8},{10,11... | collective-permute-start | bytes 393224 | tf_op jit(solution)/shard_map/ppermute | solution.py:181
  16.8 6.0 %copy-start.2 = (s32[4]{0:T(128)S(1)}, s32[4]{0:T(128)}, u32[]{:S(2)}) copy-start(s32[4]{0:T(128)} %length_ref.5) | copy-start | bytes 52
  25.1 7.8 %collective-permute-start.7 = (f32[2,1,64]{2,1,0:T(1,128)S(1)}, f32[2,1,64]{2,1,0:T(1,128)S(1)}, u32[]{:S(2)}, u32[]{:S(2)}) collective-permute-start(f32[2,1,64]{2,1,0:T(1,128)S(1)} %get-tuple-element.23), channel_id=1, source_target_pairs={{0,1},{1,0},{2,3},{3,2},{4,5},{5,4},{6,7},{7,6},{8,9},{9,8},{10,11... | collective-permute-start | bytes 1544 | tf_op jit(solution)/shard_map/ppermute | solution.py:181
  27.7 5.4 %collective-permute-start.11 = (f32[2,1,64]{2,1,0:T(1,128)S(1)}, f32[2,1,64]{2,1,0:T(1,128)S(1)}, u32[]{:S(2)}, u32[]{:S(2)}) collective-permute-start(f32[2,1,64]{2,1,0:T(1,128)S(1)} %get-tuple-element.27), channel_id=1, source_target_pairs={{0,1},{1,0},{2,3},{3,2},{4,5},{5,4},{6,7},{7,6},{8,9},{9,8},{10,11... | collective-permute-start | bytes 1544 | tf_op jit(solution)/shard_map/ppermute | solution.py:181
  28.0 16.1 %copy-start.4 = (bf16[32,512,128]{2,1,0:T(8,128)(2,1)S(1)}, bf16[32,512,128]{2,1,0:T(8,128)(2,1)}, u32[]{:S(2)}) copy-start(bf16[32,512,128]{2,1,0:T(8,128)(2,1)} %param.12) | copy-start | bytes 12582916
  32.0 4.1 %collective-permute-start.17 = (f32[4,1,64]{2,1,0:T(1,128)S(1)}, f32[4,1,64]{2,1,0:T(1,128)S(1)}, u32[]{:S(2)}, u32[]{:S(2)}) collective-permute-start(f32[4,1,64]{2,1,0:T(1,128)S(1)} %get-tuple-element.30), channel_id=1, source_target_pairs={{0,1},{1,0},{2,3},{3,2},{4,5},{5,4},{6,7},{7,6},{8,9},{9,8},{10,11... | collective-permute-start | bytes 3080 | tf_op jit(solution)/shard_map/ppermute | solution.py:181
  32.4 2.8 %collective-permute-start.8 = (bf16[2,64,512]{2,1,0:T(8,128)(2,1)S(1)}, bf16[2,64,512]{2,1,0:T(8,128)(2,1)S(1)}, u32[]{:S(2)}, u32[]{:S(2)}) collective-permute-start(bf16[2,64,512]{2,1,0:T(8,128)(2,1)S(1)} %get-tuple-element.24), channel_id=1, source_target_pairs={{0,1},{1,0},{2,3},{3,2},{4,5},{5,4},{6,7},{7,6},{8,9},{9,8},{10,11... | collective-permute-start | bytes 393224 | tf_op jit(solution)/shard_map/ppermute | solution.py:181
  32.6 2.8 %collective-permute-start.12 = (bf16[2,64,512]{2,1,0:T(8,128)(2,1)S(1)}, bf16[2,64,512]{2,1,0:T(8,128)(2,1)S(1)}, u32[]{:S(2)}, u32[]{:S(2)}) collective-permute-start(bf16[2,64,512]{2,1,0:T(8,128)(2,1)S(1)} %get-tuple-element.28), channel_id=1, source_target_pairs={{0,1},{1,0},{2,3},{3,2},{4,5},{5,4},{6,7},{7,6},{8,9},{9,8},{10,11... | collective-permute-start | bytes 393224 | tf_op jit(solution)/shard_map/ppermute | solution.py:181
  32.9 4.0 %collective-permute-start.18 = (bf16[4,64,512]{2,1,0:T(8,128)(2,1)S(1)}, bf16[4,64,512]{2,1,0:T(8,128)(2,1)S(1)}, u32[]{:S(2)}, u32[]{:S(2)}) collective-permute-start(bf16[4,64,512]{2,1,0:T(8,128)(2,1)S(1)} %get-tuple-element.32), channel_id=1, source_target_pairs={{0,1},{1,0},{2,3},{3,2},{4,5},{5,4},{6,7},{7,6},{8,9},{9,8},{10,11... | collective-permute-start | bytes 786440 | tf_op jit(solution)/shard_map/ppermute | solution.py:181
  33.1 3.7 %collective-permute-start.14 = (f32[4,1,64]{2,1,0:T(1,128)S(1)}, f32[4,1,64]{2,1,0:T(1,128)S(1)}, u32[]{:S(2)}, u32[]{:S(2)}) collective-permute-start(f32[4,1,64]{2,1,0:T(1,128)S(1)} %pad_maximum_fusion.2), channel_id=1, source_target_pairs={{0,2},{1,3},{2,0},{3,1},{4,6},{5,7},{6,4},{7,5},{8,10},{9,11},{10,... | collective-permute-start | bytes 3080 | tf_op jit(solution)/shard_map/ppermute | solution.py:181
  35.5 8.3 %collective-permute-start.13 = (bf16[4,64,512]{2,1,0:T(8,128)(2,1)S(1)}, bf16[4,64,512]{2,1,0:T(8,128)(2,1)S(1)}, u32[]{:S(2)}, u32[]{:S(2)}) collective-permute-start(bf16[4,64,512]{2,1,0:T(8,128)(2,1)S(1)} %pad_maximum_fusion), channel_id=1, source_target_pairs={{0,2},{1,3},{2,0},{3,1},{4,6},{5,7},{6,4},{7,5},{8,10},{9,11},{10,... | collective-permute-start | bytes 786440 | tf_op jit(solution)/shard_map/ppermute | solution.py:181

commit v2 on v1

--- a/solution.py
+++ b/solution.py
@@ -219,10 +219,11 @@
             after = la
             ob, lb = move(ob, 0, 1), move(lb, 0, 1)
             both = weigh([oa, ob], [la, lb])
-            joined.append(both[0].astype(bf16))
-            level.append(both[1])
-        levels.append(move(jnp.concatenate(level), -d, 0))
-        parts.append(move(jnp.concatenate(joined), -d, 0))
+            both = both[0].astype(bf16), both[1]
+            level.append(move(both[1], -d, 0))
+            joined.append(move(both[0], -d, 0))
+        levels.append(jnp.concatenate(level))
+        parts.append(jnp.concatenate(joined))
     oa, ob, la, lb = attend(
         0, lengths, own, partner, ropes[0, 0], ropes[0, 1], *cache, after, tokens, factor
     )

time: 45.7 us -> 49.6 us (1.085)
  starting transfers between devices: 13 us -> 16.6 us
    ppermute x19 -> x21, starting transfers between devices: 13 us -> 16.6 us  [move(): return lax.ppermute(x, 'tensor', pairs)]
    ppermute x19 -> x21, waiting for transfers between devices: 11.7 us -> 12.1 us  [move(): return lax.ppermute(x, 'tensor', pairs)]
  transfers between devices with their start and end apart: 19 -> 21, of which waited for: 5 -> 7; matrix products, arithmetic and copies ran while one was open for 1% -> 1% of each run, Pallas kernels for 32% -> 29%
where the time goes in v2:
time: 49.6 us; the launch traced here: 49.4 us
  starting transfers between devices  16.6 us (33%)
  Pallas kernels  14.5 us (29%)
  waiting for transfers between devices  12.1 us (24%)
  matrix products  3.59 us (7%)
  local copies, waits for them, and re-layouts  1.83 us (4%)
  other arithmetic  0.56 us (1%)
    ppermute x21, starting transfers between devices, move(): return lax.ppermute(x, 'tensor', pairs)  16.6 us
    ppermute x21, waiting for transfers between devices, move(): return lax.ppermute(x, 'tensor', pairs)  12.1 us
    pallas_call x3, Pallas kernels, attend(): pl.pallas_call(functools.partial(attend_kernel, first, tokens, factor), i...  8.56 us
    pallas_call x1, Pallas kernels, prepare(): pl.pallas_call(functools.partial(prepare_kernel, first, pieces), in_specs...  5.98 us
    dot_general x1, matrix products, local(): jnp.einsum('rthn,hnc->rthc', q_nope, w_uk, preferred_element_type=f32)  2.84 us
  transfers between devices with their start and end apart: 21, of which 7 were waited for; matrix products, arithmetic and copies ran while one was open for 1% of the time, Pallas kernels for 29%

profile of v2, /device:TPU:0, one launch (start us, length us, event | category | flops | bytes accessed | tf_op | source)
XLA Modules:
  0.0 49.4 jit_solution(2705368385316210695)
XLA Ops:
  0.0 0.8 %copy-done = bf16[4,2,32,128]{3,2,1,0:T(8,128)(2,1)S(1)} copy-done((bf16[4,2,32,128]{3,2,1,0:T(8,128)(2,1)S(1)}, bf16[4,2,32,128]{3,2,1,0:T(8,128)(2,1)}, u32[]{:S(2)}) %copy-start) | copy-done | bytes 65560
  0.8 2.8 %fusion.7 = bf16[4,2,32,512]{3,0,1,2:T(4,128)(2,1)S(1)} fusion(bf16[32,128,512]{2,1,0:T(8,128)(2,1)} %param.11, bf16[4,2,32,128]{3,2,1,0:T(8,128)(2,1)S(1)} %copy-done), kind=kOutput, calls=%fused_computation.5 | convolution fusion | flops 33685504 | bytes 4521984 | tf_op jit(solution)/shard_map/rthn,hnc->rthc/dot_general | solution.py:195
  3.7 0.2 fusion.21
  3.9 3.0 %collective-permute-start = (bf16[2,64,512]{2,1,0:T(8,128)(2,1)S(1)}, bf16[2,64,512]{2,1,0:T(8,128)(2,1)S(1)}, u32[]{:S(2)}, u32[]{:S(2)}) collective-permute-start(bf16[2,64,512]{2,1,0:T(8,128)(2,1)S(1)} %bitcast.45), channel_id=1, source_target_pairs={{0,2},{1,3},{2,0},{3,1},{4,6},{5,7},{6,4},{7,5},{8,10},{9,11},{10,... | collective-permute-start | bytes 393224 | tf_op jit(solution)/shard_map/ppermute | solution.py:181
  7.0 0.1 collective-permute-start.10
  7.1 2.0 %collective-permute-start.2 = (bf16[4,64,64]{2,1,0:T(8,128)(2,1)S(1)}, bf16[4,64,64]{2,1,0:T(8,128)(2,1)S(1)}, u32[]{:S(2)}, u32[]{:S(2)}) collective-permute-start(bf16[4,64,64]{2,1,0:T(8,128)(2,1)S(1)} %bitcast.40), channel_id=1, source_target_pairs={{0,2},{1,3},{2,0},{3,1},{4,6},{5,7},{6,4},{7,5},{8,10},{9,11},{10,... | collective-permute-start | bytes 98312 | tf_op jit(solution)/shard_map/ppermute | solution.py:181
  9.1 2.2 %collective-permute-done.qa_ref = bf16[2,64,512]{2,1,0:T(8,128)(2,1)S(1)} collective-permute-done((bf16[2,64,512]{2,1,0:T(8,128)(2,1)S(1)}, bf16[2,64,512]{2,1,0:T(8,128)(2,1)S(1)}, u32[]{:S(2)}, u32[]{:S(2)}) %collective-permute-start) | collective-permute-done | bytes 131104 | tf_op jit(solution)/shard_map/ppermute | solution.py:181
  11.3 0.0 collective-permute-start.1
  11.3 2.0 %collective-permute-start.5 = (f32[5,64]{1,0:T(8,128)S(1)}, f32[5,64]{1,0:T(8,128)S(1)}, u32[]{:S(2)}, u32[]{:S(2)}) collective-permute-start(f32[5,64]{1,0:T(8,128)S(1)} %copy-done.5), channel_id=1, source_target_pairs={{0,2},{1,3},{2,0},{3,1},{4,6},{5,7},{6,4},{7,5},{8,10},{9,11},{10,... | collective-permute-start | bytes 3848 | tf_op jit(solution)/shard_map/ppermute | solution.py:181
  13.3 0.2 collective-permute-start.4
  13.5 1.4 %collective-permute-done.5 = f32[5,64]{1,0:T(8,128)S(1)} collective-permute-done((f32[5,64]{1,0:T(8,128)S(1)}, f32[5,64]{1,0:T(8,128)S(1)}, u32[]{:S(2)}, u32[]{:S(2)}) %collective-permute-start.5) | collective-permute-done | bytes 1312 | tf_op jit(solution)/shard_map/ppermute | solution.py:181
  14.9 0.1 copy.13
  15.0 0.0 collective-permute-done.4
  15.0 0.6 %collective-permute-start.18 = (bf16[4,64,64]{2,1,0:T(8,128)(2,1)S(1)}, bf16[4,64,64]{2,1,0:T(8,128)(2,1)S(1)}, u32[]{:S(2)}, u32[]{:S(2)}) collective-permute-start(bf16[4,64,64]{2,1,0:T(8,128)(2,1)S(1)} %bitcast.41), channel_id=1, source_target_pairs={{0,1},{1,0},{2,3},{3,2},{4,5},{5,4},{6,7},{7,6},{8,9},{9,8},{10,11... | collective-permute-start | bytes 98312 | tf_op jit(solution)/shard_map/ppermute | solution.py:181
  15.6 0.5 %collective-permute-done.6 = f32[5,64]{1,0:T(8,128)S(1)} collective-permute-done((f32[5,64]{1,0:T(8,128)S(1)}, f32[5,64]{1,0:T(8,128)S(1)}, u32[]{:S(2)}, u32[]{:S(2)}) %collective-permute-start.6) | collective-permute-done | bytes 1312 | tf_op jit(solution)/shard_map/ppermute | solution.py:181
  16.1 0.2 collective-permute-start.17
  16.2 0.3 collective-permute-start.3
  16.6 0.0 collective-permute-done.10.qa_ref
  16.6 0.2 collective-permute-start.11
  16.8 0.0 copy-start.2
  16.8 6.0 %prepare.1 = (bf16[4,2048,512]{2,1,0:T(8,128)(2,1)S(1)}, bf16[4,576,2048]{2,1,0:T(8,128)(2,1)S(1)}) custom-call(s32[4,16]{1,0:T(4,128)S(1)} %copy-done.3, f32[4,5,64]{2,1,0:T(8,128)S(1)} %pad_maximum_fusion.scale_ref, bf16[4,2048,512]{2,1,0:T(8,128)(2,1)} %latent_hbm.1, bf16[4,64,2048]{2,1,0:T(8,128)(2,1)} %rope_hbm.1), custom_call_target="tpu_custom_call" | custom-call | flops 20000000 | bytes 20000000 | tf_op jit(solution)/shard_map/prepare/pallas_call | solution.py:70
  22.8 0.0 collective-permute-done.3.rb_ref
  22.8 2.3 %attend.3 = (bf16[2,64,512]{2,1,0:T(8,128)(2,1)S(1)}, bf16[2,64,512]{2,1,0:T(8,128)(2,1)S(1)}, f32[2,1,64]{2,1,0:T(1,128)S(1)}, f32[2,1,64]{2,1,0:T(1,128)S(1)}) custom-call(s32[4]{0:T(128)S(1)} %copy-done.2, bf16[2,64,512]{2,1,0:T(8,128)(2,1)S(1)} %collective-permute-done.qa_ref, bf16[2,64,512]{2,1,0:T(8,128)(2,1)S(1)} %collective-permute-done.1.qb_ref, ...), custom_call_target="tpu_custom_call" | custom-call | flops 1140850688 | bytes 4194304 | tf_op jit(solution)/shard_map/attend/pallas_call | solution.py:144
  25.1 0.4 collective-permute-start.7
  25.5 2.2 %attend.4 = (bf16[2,64,512]{2,1,0:T(8,128)(2,1)S(1)}, bf16[2,64,512]{2,1,0:T(8,128)(2,1)S(1)}, f32[2,1,64]{2,1,0:T(1,128)S(1)}, f32[2,1,64]{2,1,0:T(1,128)S(1)}) custom-call(s32[4]{0:T(128)S(1)} %copy-done.2, bf16[2,64,512]{2,1,0:T(8,128)(2,1)S(1)} %collective-permute-done.10.qa_ref, bf16[2,64,512]{2,1,0:T(8,128)(2,1)S(1)} %collective-permute-done.11.qb_ref, ...), custom_call_target="tpu_custom_call" | custom-call | flops 1140850688 | bytes 4194304 | tf_op jit(solution)/shard_map/attend/pallas_call | solution.py:144
  27.7 0.2 collective-permute-start.12
  28.0 4.0 %attend.5 = (bf16[4,64,512]{2,1,0:T(8,128)(2,1)S(1)}, bf16[4,64,512]{2,1,0:T(8,128)(2,1)S(1)}, f32[4,1,64]{2,1,0:T(1,128)S(1)}, f32[4,1,64]{2,1,0:T(1,128)S(1)}) custom-call(s32[4]{0:T(128)S(1)} %copy-done.2, bf16[4,64,512]{2,1,0:T(8,128)(2,1)S(1)} %bitcast.39, bf16[4,64,512]{2,1,0:T(8,128)(2,1)S(1)} %collective-permute-done.17.qb_ref, ...), custom_call_target="tpu_custom_call" | custom-call | flops 2281701376 | bytes 8388608 | tf_op jit(solution)/shard_map/attend/pallas_call | solution.py:144
  32.0 0.3 collective-permute-start.19
  32.4 0.2 collective-permute-start.8
  32.5 0.3 collective-permute-start.13
  32.9 0.0 collective-permute-done.7
  32.9 0.2 collective-permute-start.20
  33.1 2.1 %collective-permute-start.15 = (f32[2,1,64]{2,1,0:T(1,128)S(1)}, f32[2,1,64]{2,1,0:T(1,128)S(1)}, u32[]{:S(2)}, u32[]{:S(2)}) collective-permute-start(f32[2,1,64]{2,1,0:T(1,128)S(1)} %get-tuple-element.42), channel_id=1, source_target_pairs={{0,2},{1,3},{2,0},{3,1},{4,6},{5,7},{6,4},{7,5},{8,10},{9,11},{10,... | collective-permute-start | bytes 1544 | tf_op jit(solution)/shard_map/ppermute | solution.py:181
  35.2 1.5 %collective-permute-done.15 = f32[2,1,64]{2,1,0:T(1,128)S(1)} collective-permute-done((f32[2,1,64]{2,1,0:T(1,128)S(1)}, f32[2,1,64]{2,1,0:T(1,128)S(1)}, u32[]{:S(2)}, u32[]{:S(2)}) %collective-permute-start.15) | collective-permute-done | bytes 544 | tf_op jit(solution)/shard_map/ppermute | solution.py:181
  36.7 2.0 %collective-permute-start.16 = (f32[2,1,64]{2,1,0:T(1,128)S(1)}, f32[2,1,64]{2,1,0:T(1,128)S(1)}, u32[]{:S(2)}, u32[]{:S(2)}) collective-permute-start(f32[2,1,64]{2,1,0:T(1,128)S(1)} %get-tuple-element.39), channel_id=1, source_target_pairs={{0,2},{1,3},{2,0},{3,1},{4,6},{5,7},{6,4},{7,5},{8,10},{9,11},{10,... | collective-permute-start | bytes 1544 | tf_op jit(solution)/shard_map/ppermute | solution.py:181
  38.8 1.6 %collective-permute-done.16 = f32[2,1,64]{2,1,0:T(1,128)S(1)} collective-permute-done((f32[2,1,64]{2,1,0:T(1,128)S(1)}, f32[2,1,64]{2,1,0:T(1,128)S(1)}, u32[]{:S(2)}, u32[]{:S(2)}) %collective-permute-start.16) | collective-permute-done | bytes 544 | tf_op jit(solution)/shard_map/ppermute | solution.py:181
  40.3 0.0 collective-permute-done.8
  40.4 0.1 add_convert_fusion.2
  40.5 2.1 %collective-permute-start.9 = (bf16[2,64,512]{2,1,0:T(8,128)(2,1)S(1)}, bf16[2,64,512]{2,1,0:T(8,128)(2,1)S(1)}, u32[]{:S(2)}, u32[]{:S(2)}) collective-permute-start(bf16[2,64,512]{2,1,0:T(8,128)(2,1)S(1)} %add_convert_fusion.2), channel_id=1, source_target_pairs={{0,2},{1,3},{2,0},{3,1},{4,6},{5,7},{6,4},{7,5},{8,10},{9,11},{10,... | collective-permute-start | bytes 393224 | tf_op jit(solution)/shard_map/ppermute | solution.py:181
  42.6 0.0 collective-permute-done.13
  42.6 0.1 add_convert_fusion.1
  42.7 0.1 collective-permute-start.14
  42.8 3.1 %collective-permute-done.9 = bf16[2,64,512]{2,1,0:T(8,128)(2,1)S(1)} collective-permute-done((bf16[2,64,512]{2,1,0:T(8,128)(2,1)S(1)}, bf16[2,64,512]{2,1,0:T(8,128)(2,1)S(1)}, u32[]{:S(2)}, u32[]{:S(2)}) %collective-permute-start.9) | collective-permute-done | bytes 131104 | tf_op jit(solution)/shard_map/ppermute | solution.py:181
  45.9 1.8 %collective-permute-done.14 = bf16[2,64,512]{2,1,0:T(8,128)(2,1)S(1)} collective-permute-done((bf16[2,64,512]{2,1,0:T(8,128)(2,1)S(1)}, bf16[2,64,512]{2,1,0:T(8,128)(2,1)S(1)}, u32[]{:S(2)}, u32[]{:S(2)}) %collective-permute-start.14) | collective-permute-done | bytes 131104 | tf_op jit(solution)/shard_map/ppermute | solution.py:181
  47.7 0.0 collective-permute-done.20
  47.7 0.2 add_convert_fusion
  48.0 0.8 %fusion.13 = bf16[4,2,32,128]{3,0,1,2:T(4,128)(2,1)S(1)} fusion(bf16[32,512,128]{2,1,0:T(8,128)(2,1)S(1)} %copy-done.4, bf16[4,2,32,512]{3,2,1,0:T(8,128)(2,1)S(1)} %bitcast.43), kind=kOutput, calls=%fused_computation.7 | convolution fusion | flops 33587200 | bytes 4521984 | tf_op jit(solution)/shard_map/rthc,hcv->rthv/dot_general | solution.py:234
  48.8 0.7 %copy.15 = bf16[4,2,32,128]{3,2,1,0:T(8,128)(2,1)} copy(bf16[4,2,32,128]{3,0,1,2:T(4,128)(2,1)S(1)} %fusion.13) | data formatting | bytes 131072 | tf_op jit(solution)/shard_map/convert_element_type | solution.py:235
  (27 shorter events, 0.2 us)
Async XLA Ops:
  0.0 0.8 %copy-start = (bf16[4,2,32,128]{3,2,1,0:T(8,128)(2,1)S(1)}, bf16[4,2,32,128]{3,2,1,0:T(8,128)(2,1)}, u32[]{:S(2)}) copy-start(bf16[4,2,32,128]{3,2,1,0:T(8,128)(2,1)} %param.9) | copy-start | bytes 196612
  0.0 7.1 %copy-start.1 = (bf16[4,2,32,64]{3,2,1,0:T(8,128)(2,1)S(1)}, bf16[4,2,32,64]{3,2,1,0:T(8,128)(2,1)}, u32[]{:S(2)}) copy-start(bf16[4,2,32,64]{3,2,1,0:T(8,128)(2,1)} %param.10) | copy-start | bytes 98308
  0.0 11.3 %copy-start.5 = (f32[5,64]{1,0:T(8,128)S(1)}, f32[5,64]{1,0:T(8,128)}, u32[]{:S(2)}) copy-start(f32[5,64]{1,0:T(8,128)} %param.15) | copy-start | bytes 3844
  0.0 16.8 %copy-start.3 = (s32[4,16]{1,0:T(4,128)S(1)}, s32[4,16]{1,0:T(4,128)}, u32[]{:S(2)}) copy-start(s32[4,16]{1,0:T(4,128)} %index_ref.1) | copy-start | bytes 772
  3.9 7.4 %collective-permute-start = (bf16[2,64,512]{2,1,0:T(8,128)(2,1)S(1)}, bf16[2,64,512]{2,1,0:T(8,128)(2,1)S(1)}, u32[]{:S(2)}, u32[]{:S(2)}) collective-permute-start(bf16[2,64,512]{2,1,0:T(8,128)(2,1)S(1)} %bitcast.45), channel_id=1, source_target_pairs={{0,2},{1,3},{2,0},{3,1},{4,6},{5,7},{6,4},{7,5},{8,10},{9,11},{10,... | collective-permute-start | bytes 393224 | tf_op jit(solution)/shard_map/ppermute | solution.py:181
  7.0 9.6 %collective-permute-start.10 = (bf16[2,64,512]{2,1,0:T(8,128)(2,1)S(1)}, bf16[2,64,512]{2,1,0:T(8,128)(2,1)S(1)}, u32[]{:S(2)}, u32[]{:S(2)}) collective-permute-start(bf16[2,64,512]{2,1,0:T(8,128)(2,1)S(1)} %bitcast.44), channel_id=1, source_target_pairs={{0,2},{1,3},{2,0},{3,1},{4,6},{5,7},{6,4},{7,5},{8,10},{9,11},{10,... | collective-permute-start | bytes 393224 | tf_op jit(solution)/shard_map/ppermute | solution.py:181
  7.1 9.2 %collective-permute-start.2 = (bf16[4,64,64]{2,1,0:T(8,128)(2,1)S(1)}, bf16[4,64,64]{2,1,0:T(8,128)(2,1)S(1)}, u32[]{:S(2)}, u32[]{:S(2)}) collective-permute-start(bf16[4,64,64]{2,1,0:T(8,128)(2,1)S(1)} %bitcast.40), channel_id=1, source_target_pairs={{0,2},{1,3},{2,0},{3,1},{4,6},{5,7},{6,4},{7,5},{8,10},{9,11},{10,... | collective-permute-start | bytes 98312 | tf_op jit(solution)/shard_map/ppermute | solution.py:181
  11.3 11.5 %collective-permute-start.1 = (bf16[2,64,512]{2,1,0:T(8,128)(2,1)S(1)}, bf16[2,64,512]{2,1,0:T(8,128)(2,1)S(1)}, u32[]{:S(2)}, u32[]{:S(2)}) collective-permute-start(bf16[2,64,512]{2,1,0:T(8,128)(2,1)S(1)} %collective-permute-done.qa_ref), channel_id=1, source_target_pairs={{0,1},{1,0},{2,3},{3,2},{4,5},{5,4},{6,7},{7,6},{8,9},{9,8},{10,11... | collective-permute-start | bytes 393224 | tf_op jit(solution)/shard_map/ppermute | solution.py:181
  11.3 3.6 %collective-permute-start.5 = (f32[5,64]{1,0:T(8,128)S(1)}, f32[5,64]{1,0:T(8,128)S(1)}, u32[]{:S(2)}, u32[]{:S(2)}) collective-permute-start(f32[5,64]{1,0:T(8,128)S(1)} %copy-done.5), channel_id=1, source_target_pairs={{0,2},{1,3},{2,0},{3,1},{4,6},{5,7},{6,4},{7,5},{8,10},{9,11},{10,... | collective-permute-start | bytes 3848 | tf_op jit(solution)/shard_map/ppermute | solution.py:181
  13.3 1.7 %collective-permute-start.4 = (f32[5,64]{1,0:T(8,128)S(1)}, f32[5,64]{1,0:T(8,128)S(1)}, u32[]{:S(2)}, u32[]{:S(2)}) collective-permute-start(f32[5,64]{1,0:T(8,128)S(1)} %copy-done.5), channel_id=1, source_target_pairs={{0,1},{1,0},{2,3},{3,2},{4,5},{5,4},{6,7},{7,6},{8,9},{9,8},{10,11... | collective-permute-start | bytes 3848 | tf_op jit(solution)/shard_map/ppermute | solution.py:181
  14.9 1.2 %collective-permute-start.6 = (f32[5,64]{1,0:T(8,128)S(1)}, f32[5,64]{1,0:T(8,128)S(1)}, u32[]{:S(2)}, u32[]{:S(2)}) collective-permute-start(f32[5,64]{1,0:T(8,128)S(1)} %collective-permute-done.5), channel_id=1, source_target_pairs={{0,1},{1,0},{2,3},{3,2},{4,5},{5,4},{6,7},{7,6},{8,9},{9,8},{10,11... | collective-permute-start | bytes 3848 | tf_op jit(solution)/shard_map/ppermute | solution.py:181
  15.0 13.0 %collective-permute-start.18 = (bf16[4,64,64]{2,1,0:T(8,128)(2,1)S(1)}, bf16[4,64,64]{2,1,0:T(8,128)(2,1)S(1)}, u32[]{:S(2)}, u32[]{:S(2)}) collective-permute-start(bf16[4,64,64]{2,1,0:T(8,128)(2,1)S(1)} %bitcast.41), channel_id=1, source_target_pairs={{0,1},{1,0},{2,3},{3,2},{4,5},{5,4},{6,7},{7,6},{8,9},{9,8},{10,11... | collective-permute-start | bytes 98312 | tf_op jit(solution)/shard_map/ppermute | solution.py:181
  16.1 11.9 %collective-permute-start.17 = (bf16[4,64,512]{2,1,0:T(8,128)(2,1)S(1)}, bf16[4,64,512]{2,1,0:T(8,128)(2,1)S(1)}, u32[]{:S(2)}, u32[]{:S(2)}) collective-permute-start(bf16[4,64,512]{2,1,0:T(8,128)(2,1)S(1)} %bitcast.38), channel_id=1, source_target_pairs={{0,1},{1,0},{2,3},{3,2},{4,5},{5,4},{6,7},{7,6},{8,9},{9,8},{10,11... | collective-permute-start | bytes 786440 | tf_op jit(solution)/shard_map/ppermute | solution.py:181
  16.2 6.5 %collective-permute-start.3 = (bf16[4,64,64]{2,1,0:T(8,128)(2,1)S(1)}, bf16[4,64,64]{2,1,0:T(8,128)(2,1)S(1)}, u32[]{:S(2)}, u32[]{:S(2)}) collective-permute-start(bf16[4,64,64]{2,1,0:T(8,128)(2,1)S(1)} %collective-permute-done.2.ra_ref), channel_id=1, source_target_pairs={{0,1},{1,0},{2,3},{3,2},{4,5},{5,4},{6,7},{7,6},{8,9},{9,8},{10,11... | collective-permute-start | bytes 98312 | tf_op jit(solution)/shard_map/ppermute | solution.py:181
  16.6 8.9 %collective-permute-start.11 = (bf16[2,64,512]{2,1,0:T(8,128)(2,1)S(1)}, bf16[2,64,512]{2,1,0:T(8,128)(2,1)S(1)}, u32[]{:S(2)}, u32[]{:S(2)}) collective-permute-start(bf16[2,64,512]{2,1,0:T(8,128)(2,1)S(1)} %collective-permute-done.10.qa_ref), channel_id=1, source_target_pairs={{0,1},{1,0},{2,3},{3,2},{4,5},{5,4},{6,7},{7,6},{8,9},{9,8},{10,11... | collective-permute-start | bytes 393224 | tf_op jit(solution)/shard_map/ppermute | solution.py:181
  16.8 6.0 %copy-start.2 = (s32[4]{0:T(128)S(1)}, s32[4]{0:T(128)}, u32[]{:S(2)}) copy-start(s32[4]{0:T(128)} %length_ref.5) | copy-start | bytes 52
  25.1 7.8 %collective-permute-start.7 = (f32[2,1,64]{2,1,0:T(1,128)S(1)}, f32[2,1,64]{2,1,0:T(1,128)S(1)}, u32[]{:S(2)}, u32[]{:S(2)}) collective-permute-start(f32[2,1,64]{2,1,0:T(1,128)S(1)} %get-tuple-element.23), channel_id=1, source_target_pairs={{0,1},{1,0},{2,3},{3,2},{4,5},{5,4},{6,7},{7,6},{8,9},{9,8},{10,11... | collective-permute-start | bytes 1544 | tf_op jit(solution)/shard_map/ppermute | solution.py:181
  27.7 5.4 %collective-permute-start.12 = (f32[2,1,64]{2,1,0:T(1,128)S(1)}, f32[2,1,64]{2,1,0:T(1,128)S(1)}, u32[]{:S(2)}, u32[]{:S(2)}) collective-permute-start(f32[2,1,64]{2,1,0:T(1,128)S(1)} %get-tuple-element.27), channel_id=1, source_target_pairs={{0,1},{1,0},{2,3},{3,2},{4,5},{5,4},{6,7},{7,6},{8,9},{9,8},{10,11... | collective-permute-start | bytes 1544 | tf_op jit(solution)/shard_map/ppermute | solution.py:181
  28.0 20.0 %copy-start.4 = (bf16[32,512,128]{2,1,0:T(8,128)(2,1)S(1)}, bf16[32,512,128]{2,1,0:T(8,128)(2,1)}, u32[]{:S(2)}) copy-start(bf16[32,512,128]{2,1,0:T(8,128)(2,1)} %param.12) | copy-start | bytes 12582916
  32.0 8.3 %collective-permute-start.19 = (f32[4,1,64]{2,1,0:T(1,128)S(1)}, f32[4,1,64]{2,1,0:T(1,128)S(1)}, u32[]{:S(2)}, u32[]{:S(2)}) collective-permute-start(f32[4,1,64]{2,1,0:T(1,128)S(1)} %get-tuple-element.30), channel_id=1, source_target_pairs={{0,1},{1,0},{2,3},{3,2},{4,5},{5,4},{6,7},{7,6},{8,9},{9,8},{10,11... | collective-permute-start | bytes 3080 | tf_op jit(solution)/shard_map/ppermute | solution.py:181
  32.4 8.0 %collective-permute-start.8 = (bf16[2,64,512]{2,1,0:T(8,128)(2,1)S(1)}, bf16[2,64,512]{2,1,0:T(8,128)(2,1)S(1)}, u32[]{:S(2)}, u32[]{:S(2)}) collective-permute-start(bf16[2,64,512]{2,1,0:T(8,128)(2,1)S(1)} %get-tuple-element.24), channel_id=1, source_target_pairs={{0,1},{1,0},{2,3},{3,2},{4,5},{5,4},{6,7},{7,6},{8,9},{9,8},{10,11... | collective-permute-start | bytes 393224 | tf_op jit(solution)/shard_map/ppermute | solution.py:181
  32.5 10.0 %collective-permute-start.13 = (bf16[2,64,512]{2,1,0:T(8,128)(2,1)S(1)}, bf16[2,64,512]{2,1,0:T(8,128)(2,1)S(1)}, u32[]{:S(2)}, u32[]{:S(2)}) collective-permute-start(bf16[2,64,512]{2,1,0:T(8,128)(2,1)S(1)} %get-tuple-element.28), channel_id=1, source_target_pairs={{0,1},{1,0},{2,3},{3,2},{4,5},{5,4},{6,7},{7,6},{8,9},{9,8},{10,11... | collective-permute-start | bytes 393224 | tf_op jit(solution)/shard_map/ppermute | solution.py:181
  32.9 14.8 %collective-permute-start.20 = (bf16[4,64,512]{2,1,0:T(8,128)(2,1)S(1)}, bf16[4,64,512]{2,1,0:T(8,128)(2,1)S(1)}, u32[]{:S(2)}, u32[]{:S(2)}) collective-permute-start(bf16[4,64,512]{2,1,0:T(8,128)(2,1)S(1)} %get-tuple-element.32), channel_id=1, source_target_pairs={{0,1},{1,0},{2,3},{3,2},{4,5},{5,4},{6,7},{7,6},{8,9},{9,8},{10,11... | collective-permute-start | bytes 786440 | tf_op jit(solution)/shard_map/ppermute | solution.py:181
  33.1 3.6 %collective-permute-start.15 = (f32[2,1,64]{2,1,0:T(1,128)S(1)}, f32[2,1,64]{2,1,0:T(1,128)S(1)}, u32[]{:S(2)}, u32[]{:S(2)}) collective-permute-start(f32[2,1,64]{2,1,0:T(1,128)S(1)} %get-tuple-element.42), channel_id=1, source_target_pairs={{0,2},{1,3},{2,0},{3,1},{4,6},{5,7},{6,4},{7,5},{8,10},{9,11},{10,... | collective-permute-start | bytes 1544 | tf_op jit(solution)/shard_map/ppermute | solution.py:181
  36.7 3.6 %collective-permute-start.16 = (f32[2,1,64]{2,1,0:T(1,128)S(1)}, f32[2,1,64]{2,1,0:T(1,128)S(1)}, u32[]{:S(2)}, u32[]{:S(2)}) collective-permute-start(f32[2,1,64]{2,1,0:T(1,128)S(1)} %get-tuple-element.39), channel_id=1, source_target_pairs={{0,2},{1,3},{2,0},{3,1},{4,6},{5,7},{6,4},{7,5},{8,10},{9,11},{10,... | collective-permute-start | bytes 1544 | tf_op jit(solution)/shard_map/ppermute | solution.py:181
  40.5 5.4 %collective-permute-start.9 = (bf16[2,64,512]{2,1,0:T(8,128)(2,1)S(1)}, bf16[2,64,512]{2,1,0:T(8,128)(2,1)S(1)}, u32[]{:S(2)}, u32[]{:S(2)}) collective-permute-start(bf16[2,64,512]{2,1,0:T(8,128)(2,1)S(1)} %add_convert_fusion.2), channel_id=1, source_target_pairs={{0,2},{1,3},{2,0},{3,1},{4,6},{5,7},{6,4},{7,5},{8,10},{9,11},{10,... | collective-permute-start | bytes 393224 | tf_op jit(solution)/shard_map/ppermute | solution.py:181
  42.7 5.0 %collective-permute-start.14 = (bf16[2,64,512]{2,1,0:T(8,128)(2,1)S(1)}, bf16[2,64,512]{2,1,0:T(8,128)(2,1)S(1)}, u32[]{:S(2)}, u32[]{:S(2)}) collective-permute-start(bf16[2,64,512]{2,1,0:T(8,128)(2,1)S(1)} %add_convert_fusion.1), channel_id=1, source_target_pairs={{0,2},{1,3},{2,0},{3,1},{4,6},{5,7},{6,4},{7,5},{8,10},{9,11},{10,... | collective-permute-start | bytes 393224 | tf_op jit(solution)/shard_map/ppermute | solution.py:181

commit v3 on v1

--- a/solution.py
+++ b/solution.py
@@ -156,15 +156,82 @@
     )(lengths, qa, qb, ra, rb, key, turned, after)
 
 
-def weigh(parts, levels):
+def joined(parts, levels):
+    rows, width = parts[0].shape
     top = functools.reduce(jnp.maximum, levels)
     shares = [jnp.exp2(level - top) for level in levels]
     total = functools.reduce(jnp.add, shares)
-    columns = [jnp.swapaxes(share / total, 1, 2) for share in shares]
-    joined = functools.reduce(
-        jnp.add, [part.astype(f32) * column for part, column in zip(parts, columns)]
-    )
-    return joined, top + jnp.log2(total)
+    mixed = None
+    for part, share in zip(parts, shares):
+        row = share / total
+        if rows < 128:
+            row = jnp.concatenate([row, jnp.zeros((1, 128 - rows), f32)], axis=1)
+        column = jnp.broadcast_to(row, (128, row.shape[1])).T[:rows]
+        term = part.astype(f32) * jnp.concatenate([column] * (width // 128), axis=1)
+        mixed = term if mixed is None else mixed + term
+    return mixed.astype(bf16), top + jnp.log2(total)
+
+
+def weigh_kernel(oa_ref, ob_ref, la_ref, lb_ref, out_ref):
+    requests, rows, width = oa_ref.shape
+    levels = []
+    for r in range(requests):
+        mixed, level = joined([oa_ref[r], ob_ref[r]], [la_ref[r], lb_ref[r]])
+        out_ref[r * rows : (r + 1) * rows] = mixed
+        levels.append(level)
+    rest = jnp.concatenate(levels, axis=1)
+    count = requests * rows
+    terms = []
+    for _ in range(3):
+        terms.append(rest.astype(bf16).astype(f32))
+        rest = rest - terms[-1]
+    terms = jnp.concatenate(terms + [jnp.zeros((5, count), f32)], axis=0)
+    if count < width:
+        terms = jnp.concatenate([terms, jnp.zeros((8, width - count), f32)], axis=1)
+    out_ref[count:] = terms.astype(bf16)
+
+
+def weigh(oa, ob, la, lb):
+    requests, rows, width = oa.shape
+    return pl.pallas_call(
+        weigh_kernel,
+        in_specs=[VMEM] * 4,
+        out_specs=VMEM,
+        out_shape=jax.ShapeDtypeStruct((requests * rows + 8, width), bf16),
+        compiler_params=pltpu.CompilerParams(vmem_limit_bytes=6 << 20),
+        cost_estimate=pl.CostEstimate(flops=200_000, bytes_accessed=500_000, transcendentals=1000),
+        name="weigh",
+    )(oa, ob, la, lb)
+
+
+def finish_kernel(half, oa_ref, ob_ref, la_ref, lb_ref, *refs):
+    out_ref, backs = refs[-1], refs[:-1]
+    requests, rows, _ = oa_ref.shape
+    count = half * rows
+    pieces = requests // half
+    levels = []
+    for back in backs:
+        terms = back[count : count + 8].astype(f32)
+        levels.append((terms[0:1] + terms[1:2]) + terms[2:3])
+    for r in range(requests):
+        h, i = divmod(r, half)
+        at = slice(i * rows, (i + 1) * rows)
+        out_ref[r] = joined(
+            [oa_ref[r], ob_ref[r]] + [back[at] for back in backs[h::pieces]],
+            [la_ref[r], lb_ref[r]] + [level[:, at] for level in levels[h::pieces]],
+        )[0]
+
+
+def finish(half, oa, ob, la, lb, backs):
+    return pl.pallas_call(
+        functools.partial(finish_kernel, half),
+        in_specs=[VMEM] * (4 + len(backs)),
+        out_specs=VMEM,
+        out_shape=jax.ShapeDtypeStruct(oa.shape, bf16),
+        compiler_params=pltpu.CompilerParams(vmem_limit_bytes=6 << 20),
+        cost_estimate=pl.CostEstimate(flops=500_000, bytes_accessed=1_000_000, transcendentals=2000),
+        name="finish",
+    )(oa, ob, la, lb, *backs)
 
 
 def local(tensor, q_nope, q_rope, w_uk, w_uv, cache_latent, cache_rope, scale_pool, block_index, lengths):
@@ -209,26 +276,20 @@
     table = jnp.stack(list(scales.values()))
     cache = prepare(0, requests, block_index, table, cache_latent, cache_rope)
     after = lengths
-    parts, levels = [], []
+    backs = []
     for d in range(1, chips):
-        joined, level = [], []
         for h in range(len(halves)):
             oa, ob, la, lb = attend(
                 h * half, lengths, query[h][d, 0], query[h][d, 1], ropes[d, 0], ropes[d, 1], *cache, after, tokens, factor
             )
             after = la
             ob, lb = move(ob, 0, 1), move(lb, 0, 1)
-            both = weigh([oa, ob], [la, lb])
-            joined.append(both[0].astype(bf16))
-            level.append(both[1])
-        levels.append(move(jnp.concatenate(level), -d, 0))
-        parts.append(move(jnp.concatenate(joined), -d, 0))
+            both = weigh(oa, ob, la, lb)
+            backs.append(move(both, -d, 0))
     oa, ob, la, lb = attend(
         0, lengths, own, partner, ropes[0, 0], ropes[0, 1], *cache, after, tokens, factor
     )
-    parts += [oa, move(ob, 0, 1)]
-    levels += [la, move(lb, 0, 1)]
-    attended = weigh(parts, levels)[0].astype(bf16)
+    attended = finish(half, oa, move(ob, 0, 1), la, move(lb, 0, 1), backs)
     attended = attended.reshape(requests, tokens, heads, width)
     projected = jnp.einsum("rthc,hcv->rthv", attended, w_uv, preferred_element_type=f32)
     return projected.astype(bf16)

time: 45.7 us -> 45.1 us (0.987)
  Pallas kernels: 14.6 us -> 15.4 us
  starting transfers between devices: 13 us -> 12.3 us
  other arithmetic: 0.6 us -> 0.01 us
    pallas_call x0 -> x3, Pallas kernels: none -> 0.83 us  [the longest x1 0.52 us: finish(): pl.pallas_call(functools.partial(finish_kernel, half), in_specs=[VMEM] *...]
    ppermute x19, starting transfers between devices: 13 us -> 12.3 us  [move(): return lax.ppermute(x, 'tensor', pairs)]
    convert_element_type x3 -> x0, other arithmetic: 0.47 us -> none  [the longest x1 0.24 us: local(): attended = weigh(parts, levels)[0].astype(bf16)]
  transfers between devices with their start and end apart: 19 -> 19, of which waited for: 5 -> 7; matrix products, arithmetic and copies ran while one was open for 1% -> 0% of each run, Pallas kernels for 32% -> 33%
where the time goes in v3:
time: 45.1 us; the launch traced here: 44.9 us
  Pallas kernels  15.4 us (34%)
  starting transfers between devices  12.3 us (27%)
  waiting for transfers between devices  11.6 us (26%)
  matrix products  3.59 us (8%)
  local copies, waits for them, and re-layouts  1.82 us (4%)
    ppermute x19, starting transfers between devices, move(): return lax.ppermute(x, 'tensor', pairs)  12.3 us
    ppermute x19, waiting for transfers between devices, move(): return lax.ppermute(x, 'tensor', pairs)  11.6 us
    pallas_call x3, Pallas kernels, attend(): pl.pallas_call(functools.partial(attend_kernel, first, tokens, factor), i...  8.58 us
    pallas_call x1, Pallas kernels, prepare(): pl.pallas_call(functools.partial(prepare_kernel, first, pieces), in_specs...  5.98 us
    dot_general x1, matrix products, local(): jnp.einsum('rthn,hnc->rthc', q_nope, w_uk, preferred_element_type=f32)  2.84 us
  transfers between devices with their start and end apart: 19, of which 7 were waited for; matrix products, arithmetic and copies ran while one was open for 0% of the time, Pallas kernels for 33%

profile of v3, /device:TPU:0, one launch (start us, length us, event | category | flops | bytes accessed | tf_op | source)
XLA Modules:
  0.0 44.9 jit_solution(8790459115366984808)
XLA Ops:
  0.0 0.8 %copy-done = bf16[4,2,32,128]{3,2,1,0:T(8,128)(2,1)S(1)} copy-done((bf16[4,2,32,128]{3,2,1,0:T(8,128)(2,1)S(1)}, bf16[4,2,32,128]{3,2,1,0:T(8,128)(2,1)}, u32[]{:S(2)}) %copy-start) | copy-done | bytes 65560
  0.8 2.8 %fusion.7 = bf16[4,2,32,512]{3,0,1,2:T(4,128)(2,1)S(1)} fusion(bf16[32,128,512]{2,1,0:T(8,128)(2,1)} %param.11, bf16[4,2,32,128]{3,2,1,0:T(8,128)(2,1)S(1)} %copy-done), kind=kOutput, calls=%fused_computation.5 | convolution fusion | flops 33685504 | bytes 4521984 | tf_op jit(solution)/shard_map/rthn,hnc->rthc/dot_general | solution.py:262
  3.7 0.2 fusion.18
  3.9 3.0 %collective-permute-start.9 = (bf16[2,64,512]{2,1,0:T(8,128)(2,1)S(1)}, bf16[2,64,512]{2,1,0:T(8,128)(2,1)S(1)}, u32[]{:S(2)}, u32[]{:S(2)}) collective-permute-start(bf16[2,64,512]{2,1,0:T(8,128)(2,1)S(1)} %bitcast.38), channel_id=1, source_target_pairs={{0,2},{1,3},{2,0},{3,1},{4,6},{5,7},{6,4},{7,5},{8,10},{9,11},{10,... | collective-permute-start | bytes 393224 | tf_op jit(solution)/shard_map/ppermute | solution.py:248
  7.0 0.1 collective-permute-start.5
  7.1 2.0 %collective-permute-start.7 = (bf16[4,64,64]{2,1,0:T(8,128)(2,1)S(1)}, bf16[4,64,64]{2,1,0:T(8,128)(2,1)S(1)}, u32[]{:S(2)}, u32[]{:S(2)}) collective-permute-start(bf16[4,64,64]{2,1,0:T(8,128)(2,1)S(1)} %bitcast.34), channel_id=1, source_target_pairs={{0,2},{1,3},{2,0},{3,1},{4,6},{5,7},{6,4},{7,5},{8,10},{9,11},{10,... | collective-permute-start | bytes 98312 | tf_op jit(solution)/shard_map/ppermute | solution.py:248
  9.1 2.2 %collective-permute-done.9.qa_ref = bf16[2,64,512]{2,1,0:T(8,128)(2,1)S(1)} collective-permute-done((bf16[2,64,512]{2,1,0:T(8,128)(2,1)S(1)}, bf16[2,64,512]{2,1,0:T(8,128)(2,1)S(1)}, u32[]{:S(2)}, u32[]{:S(2)}) %collective-permute-start.9) | collective-permute-done | bytes 131104 | tf_op jit(solution)/shard_map/ppermute | solution.py:248
  11.3 0.0 collective-permute-start.10
  11.3 2.0 %collective-permute-start.3 = (f32[5,64]{1,0:T(8,128)S(1)}, f32[5,64]{1,0:T(8,128)S(1)}, u32[]{:S(2)}, u32[]{:S(2)}) collective-permute-start(f32[5,64]{1,0:T(8,128)S(1)} %copy-done.5), channel_id=1, source_target_pairs={{0,2},{1,3},{2,0},{3,1},{4,6},{5,7},{6,4},{7,5},{8,10},{9,11},{10,... | collective-permute-start | bytes 3848 | tf_op jit(solution)/shard_map/ppermute | solution.py:248
  13.3 0.2 collective-permute-start.2
  13.5 1.4 %collective-permute-done.3 = f32[5,64]{1,0:T(8,128)S(1)} collective-permute-done((f32[5,64]{1,0:T(8,128)S(1)}, f32[5,64]{1,0:T(8,128)S(1)}, u32[]{:S(2)}, u32[]{:S(2)}) %collective-permute-start.3) | collective-permute-done | bytes 1312 | tf_op jit(solution)/shard_map/ppermute | solution.py:248
  14.9 0.0 collective-permute-start.4
  14.9 0.1 copy.11
  15.0 0.0 collective-permute-done.2
  15.0 0.6 %collective-permute-start.1 = (bf16[4,64,64]{2,1,0:T(8,128)(2,1)S(1)}, bf16[4,64,64]{2,1,0:T(8,128)(2,1)S(1)}, u32[]{:S(2)}, u32[]{:S(2)}) collective-permute-start(bf16[4,64,64]{2,1,0:T(8,128)(2,1)S(1)} %bitcast.35), channel_id=1, source_target_pairs={{0,1},{1,0},{2,3},{3,2},{4,5},{5,4},{6,7},{7,6},{8,9},{9,8},{10,11... | collective-permute-start | bytes 98312 | tf_op jit(solution)/shard_map/ppermute | solution.py:248
  15.6 0.5 %collective-permute-done.4 = f32[5,64]{1,0:T(8,128)S(1)} collective-permute-done((f32[5,64]{1,0:T(8,128)S(1)}, f32[5,64]{1,0:T(8,128)S(1)}, u32[]{:S(2)}, u32[]{:S(2)}) %collective-permute-start.4) | collective-permute-done | bytes 1312 | tf_op jit(solution)/shard_map/ppermute | solution.py:248
  16.1 0.2 collective-permute-start
  16.2 0.3 collective-permute-start.8
  16.6 0.0 collective-permute-done.5.qa_ref
  16.6 0.2 collective-permute-start.6
  16.8 0.0 copy-start.2
  16.8 6.0 %prepare.1 = (bf16[4,2048,512]{2,1,0:T(8,128)(2,1)S(1)}, bf16[4,576,2048]{2,1,0:T(8,128)(2,1)S(1)}) custom-call(s32[4,16]{1,0:T(4,128)S(1)} %copy-done.3, f32[4,5,64]{2,1,0:T(8,128)S(1)} %pad_maximum_fusion.scale_ref, bf16[4,2048,512]{2,1,0:T(8,128)(2,1)} %latent_hbm.1, bf16[4,64,2048]{2,1,0:T(8,128)(2,1)} %rope_hbm.1), custom_call_target="tpu_custom_call" | custom-call | flops 20000000 | bytes 20000000 | tf_op jit(solution)/shard_map/prepare/pallas_call | solution.py:70
  22.8 0.0 collective-permute-done.8.rb_ref
  22.8 2.3 %attend.3 = (bf16[2,64,512]{2,1,0:T(8,128)(2,1)S(1)}, bf16[2,64,512]{2,1,0:T(8,128)(2,1)S(1)}, f32[2,1,64]{2,1,0:T(1,128)S(1)}, f32[2,1,64]{2,1,0:T(1,128)S(1)}) custom-call(s32[4]{0:T(128)S(1)} %copy-done.2, bf16[2,64,512]{2,1,0:T(8,128)(2,1)S(1)} %collective-permute-done.9.qa_ref, bf16[2,64,512]{2,1,0:T(8,128)(2,1)S(1)} %collective-permute-done.10.qb_ref, ...), custom_call_target="tpu_custom_call" | custom-call | flops 1140850688 | bytes 4194304 | tf_op jit(solution)/shard_map/attend/pallas_call | solution.py:144
  25.1 2.2 %attend.4 = (bf16[2,64,512]{2,1,0:T(8,128)(2,1)S(1)}, bf16[2,64,512]{2,1,0:T(8,128)(2,1)S(1)}, f32[2,1,64]{2,1,0:T(1,128)S(1)}, f32[2,1,64]{2,1,0:T(1,128)S(1)}) custom-call(s32[4]{0:T(128)S(1)} %copy-done.2, bf16[2,64,512]{2,1,0:T(8,128)(2,1)S(1)} %collective-permute-done.5.qa_ref, bf16[2,64,512]{2,1,0:T(8,128)(2,1)S(1)} %collective-permute-done.6.qb_ref, ...), custom_call_target="tpu_custom_call" | custom-call | flops 1140850688 | bytes 4194304 | tf_op jit(solution)/shard_map/attend/pallas_call | solution.py:144
  27.3 0.4 collective-permute-start.16
  27.7 0.2 collective-permute-start.13
  27.9 0.0 collective-permute-done.1.rb_ref
  27.9 0.0 collective-permute-done.qb_ref
  27.9 4.1 %attend.5 = (bf16[4,64,512]{2,1,0:T(8,128)(2,1)S(1)}, bf16[4,64,512]{2,1,0:T(8,128)(2,1)S(1)}, f32[4,1,64]{2,1,0:T(1,128)S(1)}, f32[4,1,64]{2,1,0:T(1,128)S(1)}) custom-call(s32[4]{0:T(128)S(1)} %copy-done.2, bf16[4,64,512]{2,1,0:T(8,128)(2,1)S(1)} %bitcast.32, bf16[4,64,512]{2,1,0:T(8,128)(2,1)S(1)} %collective-permute-done.qb_ref, ...), custom_call_target="tpu_custom_call" | custom-call | flops 2281701376 | bytes 8388608 | tf_op jit(solution)/shard_map/attend/pallas_call | solution.py:144
  32.0 0.3 collective-permute-start.11
  32.3 0.2 collective-permute-start.17
  32.5 0.3 collective-permute-start.14
  32.8 0.7 %collective-permute-done.17.lb_ref = f32[2,1,64]{2,1,0:T(1,128)S(1)} collective-permute-done((f32[2,1,64]{2,1,0:T(1,128)S(1)}, f32[2,1,64]{2,1,0:T(1,128)S(1)}, u32[]{:S(2)}, u32[]{:S(2)}) %collective-permute-start.17) | collective-permute-done | bytes 544 | tf_op jit(solution)/shard_map/ppermute | solution.py:248
  33.5 0.0 collective-permute-done.16.ob_ref
  33.5 0.2 weigh.3
  33.7 2.1 %collective-permute-start.18 = (bf16[136,512]{1,0:T(8,128)(2,1)S(1)}, bf16[136,512]{1,0:T(8,128)(2,1)S(1)}, u32[]{:S(2)}, u32[]{:S(2)}) collective-permute-start(bf16[136,512]{1,0:T(8,128)(2,1)S(1)} %weigh.3), channel_id=1, source_target_pairs={{0,2},{1,3},{2,0},{3,1},{4,6},{5,7},{6,4},{7,5},{8,10},{9,11},{10,... | collective-permute-start | bytes 417800 | tf_op jit(solution)/shard_map/ppermute | solution.py:248
  35.8 0.0 collective-permute-done.14.lb_ref
  35.8 0.0 collective-permute-done.13.ob_ref
  35.8 0.2 weigh.2
  35.9 0.1 collective-permute-start.15
  36.0 0.1 collective-permute-start.12
  36.1 1.1 %collective-permute-done.12.lb_ref = f32[4,1,64]{2,1,0:T(1,128)S(1)} collective-permute-done((f32[4,1,64]{2,1,0:T(1,128)S(1)}, f32[4,1,64]{2,1,0:T(1,128)S(1)}, u32[]{:S(2)}, u32[]{:S(2)}) %collective-permute-start.12) | collective-permute-done | bytes 1056 | tf_op jit(solution)/shard_map/ppermute | solution.py:248
  37.2 3.1 %collective-permute-done.18.refs_1_ = bf16[136,512]{1,0:T(8,128)(2,1)S(1)} collective-permute-done((bf16[136,512]{1,0:T(8,128)(2,1)S(1)}, bf16[136,512]{1,0:T(8,128)(2,1)S(1)}, u32[]{:S(2)}, u32[]{:S(2)}) %collective-permute-start.18) | collective-permute-done | bytes 139296 | tf_op jit(solution)/shard_map/ppermute | solution.py:248
  40.3 2.6 %collective-permute-done.15.refs_0_ = bf16[136,512]{1,0:T(8,128)(2,1)S(1)} collective-permute-done((bf16[136,512]{1,0:T(8,128)(2,1)S(1)}, bf16[136,512]{1,0:T(8,128)(2,1)S(1)}, u32[]{:S(2)}, u32[]{:S(2)}) %collective-permute-start.15) | collective-permute-done | bytes 139296 | tf_op jit(solution)/shard_map/ppermute | solution.py:248
  42.9 0.5 %finish.1 = bf16[4,64,512]{2,1,0:T(8,128)(2,1)S(1)} custom-call(bf16[4,64,512]{2,1,0:T(8,128)(2,1)S(1)} %get-tuple-element.23.oa_ref, bf16[4,64,512]{2,1,0:T(8,128)(2,1)S(1)} %collective-permute-done.11.ob_ref, f32[4,1,64]{2,1,0:T(1,128)S(1)} %get-tuple-element.25.la_ref, f32[4,1,64]{2,1,0:T(1,128)S(1)} %collective-permute-done.12.lb_ref, ...), custom_call_target="tpu_custom_call" | custom-call | flops 500000 | bytes 1000000 | tf_op jit(solution)/shard_map/finish/pallas_call | solution.py:226
  43.5 0.8 %fusion.13 = bf16[4,2,32,128]{3,0,1,2:T(4,128)(2,1)S(1)} fusion(bf16[32,512,128]{2,1,0:T(8,128)(2,1)S(1)} %copy-done.4, bf16[4,2,32,512]{3,2,1,0:T(8,128)(2,1)S(1)} %bitcast.33), kind=kOutput, calls=%fused_computation.7 | convolution fusion | flops 33587200 | bytes 4521984 | tf_op jit(solution)/shard_map/rthc,hcv->rthv/dot_general | solution.py:294
  44.2 0.7 %copy.15 = bf16[4,2,32,128]{3,2,1,0:T(8,128)(2,1)} copy(bf16[4,2,32,128]{3,0,1,2:T(4,128)(2,1)S(1)} %fusion.13) | data formatting | bytes 131072 | tf_op jit(solution)/shard_map/convert_element_type | solution.py:295
  (17 shorter events, 0.1 us)
Async XLA Ops:
  0.0 0.8 %copy-start = (bf16[4,2,32,128]{3,2,1,0:T(8,128)(2,1)S(1)}, bf16[4,2,32,128]{3,2,1,0:T(8,128)(2,1)}, u32[]{:S(2)}) copy-start(bf16[4,2,32,128]{3,2,1,0:T(8,128)(2,1)} %param.9) | copy-start | bytes 196612
  0.0 7.1 %copy-start.1 = (bf16[4,2,32,64]{3,2,1,0:T(8,128)(2,1)S(1)}, bf16[4,2,32,64]{3,2,1,0:T(8,128)(2,1)}, u32[]{:S(2)}) copy-start(bf16[4,2,32,64]{3,2,1,0:T(8,128)(2,1)} %param.10) | copy-start | bytes 98308
  0.0 11.3 %copy-start.5 = (f32[5,64]{1,0:T(8,128)S(1)}, f32[5,64]{1,0:T(8,128)}, u32[]{:S(2)}) copy-start(f32[5,64]{1,0:T(8,128)} %param.15) | copy-start | bytes 3844
  0.0 16.8 %copy-start.3 = (s32[4,16]{1,0:T(4,128)S(1)}, s32[4,16]{1,0:T(4,128)}, u32[]{:S(2)}) copy-start(s32[4,16]{1,0:T(4,128)} %index_ref.1) | copy-start | bytes 772
  3.9 7.4 %collective-permute-start.9 = (bf16[2,64,512]{2,1,0:T(8,128)(2,1)S(1)}, bf16[2,64,512]{2,1,0:T(8,128)(2,1)S(1)}, u32[]{:S(2)}, u32[]{:S(2)}) collective-permute-start(bf16[2,64,512]{2,1,0:T(8,128)(2,1)S(1)} %bitcast.38), channel_id=1, source_target_pairs={{0,2},{1,3},{2,0},{3,1},{4,6},{5,7},{6,4},{7,5},{8,10},{9,11},{10,... | collective-permute-start | bytes 393224 | tf_op jit(solution)/shard_map/ppermute | solution.py:248
  7.0 9.6 %collective-permute-start.5 = (bf16[2,64,512]{2,1,0:T(8,128)(2,1)S(1)}, bf16[2,64,512]{2,1,0:T(8,128)(2,1)S(1)}, u32[]{:S(2)}, u32[]{:S(2)}) collective-permute-start(bf16[2,64,512]{2,1,0:T(8,128)(2,1)S(1)} %bitcast.37), channel_id=1, source_target_pairs={{0,2},{1,3},{2,0},{3,1},{4,6},{5,7},{6,4},{7,5},{8,10},{9,11},{10,... | collective-permute-start | bytes 393224 | tf_op jit(solution)/shard_map/ppermute | solution.py:248
  7.1 9.2 %collective-permute-start.7 = (bf16[4,64,64]{2,1,0:T(8,128)(2,1)S(1)}, bf16[4,64,64]{2,1,0:T(8,128)(2,1)S(1)}, u32[]{:S(2)}, u32[]{:S(2)}) collective-permute-start(bf16[4,64,64]{2,1,0:T(8,128)(2,1)S(1)} %bitcast.34), channel_id=1, source_target_pairs={{0,2},{1,3},{2,0},{3,1},{4,6},{5,7},{6,4},{7,5},{8,10},{9,11},{10,... | collective-permute-start | bytes 98312 | tf_op jit(solution)/shard_map/ppermute | solution.py:248
  11.3 11.5 %collective-permute-start.10 = (bf16[2,64,512]{2,1,0:T(8,128)(2,1)S(1)}, bf16[2,64,512]{2,1,0:T(8,128)(2,1)S(1)}, u32[]{:S(2)}, u32[]{:S(2)}) collective-permute-start(bf16[2,64,512]{2,1,0:T(8,128)(2,1)S(1)} %collective-permute-done.9.qa_ref), channel_id=1, source_target_pairs={{0,1},{1,0},{2,3},{3,2},{4,5},{5,4},{6,7},{7,6},{8,9},{9,8},{10,11... | collective-permute-start | bytes 393224 | tf_op jit(solution)/shard_map/ppermute | solution.py:248
  11.3 3.6 %collective-permute-start.3 = (f32[5,64]{1,0:T(8,128)S(1)}, f32[5,64]{1,0:T(8,128)S(1)}, u32[]{:S(2)}, u32[]{:S(2)}) collective-permute-start(f32[5,64]{1,0:T(8,128)S(1)} %copy-done.5), channel_id=1, source_target_pairs={{0,2},{1,3},{2,0},{3,1},{4,6},{5,7},{6,4},{7,5},{8,10},{9,11},{10,... | collective-permute-start | bytes 3848 | tf_op jit(solution)/shard_map/ppermute | solution.py:248
  13.3 1.7 %collective-permute-start.2 = (f32[5,64]{1,0:T(8,128)S(1)}, f32[5,64]{1,0:T(8,128)S(1)}, u32[]{:S(2)}, u32[]{:S(2)}) collective-permute-start(f32[5,64]{1,0:T(8,128)S(1)} %copy-done.5), channel_id=1, source_target_pairs={{0,1},{1,0},{2,3},{3,2},{4,5},{5,4},{6,7},{7,6},{8,9},{9,8},{10,11... | collective-permute-start | bytes 3848 | tf_op jit(solution)/shard_map/ppermute | solution.py:248
  14.9 1.2 %collective-permute-start.4 = (f32[5,64]{1,0:T(8,128)S(1)}, f32[5,64]{1,0:T(8,128)S(1)}, u32[]{:S(2)}, u32[]{:S(2)}) collective-permute-start(f32[5,64]{1,0:T(8,128)S(1)} %collective-permute-done.3), channel_id=1, source_target_pairs={{0,1},{1,0},{2,3},{3,2},{4,5},{5,4},{6,7},{7,6},{8,9},{9,8},{10,11... | collective-permute-start | bytes 3848 | tf_op jit(solution)/shard_map/ppermute | solution.py:248
  15.0 12.9 %collective-permute-start.1 = (bf16[4,64,64]{2,1,0:T(8,128)(2,1)S(1)}, bf16[4,64,64]{2,1,0:T(8,128)(2,1)S(1)}, u32[]{:S(2)}, u32[]{:S(2)}) collective-permute-start(bf16[4,64,64]{2,1,0:T(8,128)(2,1)S(1)} %bitcast.35), channel_id=1, source_target_pairs={{0,1},{1,0},{2,3},{3,2},{4,5},{5,4},{6,7},{7,6},{8,9},{9,8},{10,11... | collective-permute-start | bytes 98312 | tf_op jit(solution)/shard_map/ppermute | solution.py:248
  16.1 11.9 %collective-permute-start = (bf16[4,64,512]{2,1,0:T(8,128)(2,1)S(1)}, bf16[4,64,512]{2,1,0:T(8,128)(2,1)S(1)}, u32[]{:S(2)}, u32[]{:S(2)}) collective-permute-start(bf16[4,64,512]{2,1,0:T(8,128)(2,1)S(1)} %bitcast.31), channel_id=1, source_target_pairs={{0,1},{1,0},{2,3},{3,2},{4,5},{5,4},{6,7},{7,6},{8,9},{9,8},{10,11... | collective-permute-start | bytes 786440 | tf_op jit(solution)/shard_map/ppermute | solution.py:248
  16.2 6.5 %collective-permute-start.8 = (bf16[4,64,64]{2,1,0:T(8,128)(2,1)S(1)}, bf16[4,64,64]{2,1,0:T(8,128)(2,1)S(1)}, u32[]{:S(2)}, u32[]{:S(2)}) collective-permute-start(bf16[4,64,64]{2,1,0:T(8,128)(2,1)S(1)} %collective-permute-done.7.ra_ref), channel_id=1, source_target_pairs={{0,1},{1,0},{2,3},{3,2},{4,5},{5,4},{6,7},{7,6},{8,9},{9,8},{10,11... | collective-permute-start | bytes 98312 | tf_op jit(solution)/shard_map/ppermute | solution.py:248
  16.6 8.5 %collective-permute-start.6 = (bf16[2,64,512]{2,1,0:T(8,128)(2,1)S(1)}, bf16[2,64,512]{2,1,0:T(8,128)(2,1)S(1)}, u32[]{:S(2)}, u32[]{:S(2)}) collective-permute-start(bf16[2,64,512]{2,1,0:T(8,128)(2,1)S(1)} %collective-permute-done.5.qa_ref), channel_id=1, source_target_pairs={{0,1},{1,0},{2,3},{3,2},{4,5},{5,4},{6,7},{7,6},{8,9},{9,8},{10,11... | collective-permute-start | bytes 393224 | tf_op jit(solution)/shard_map/ppermute | solution.py:248
  16.8 6.0 %copy-start.2 = (s32[4]{0:T(128)S(1)}, s32[4]{0:T(128)}, u32[]{:S(2)}) copy-start(s32[4]{0:T(128)} %length_ref.5) | copy-start | bytes 52
  27.3 6.2 %collective-permute-start.16 = (bf16[2,64,512]{2,1,0:T(8,128)(2,1)S(1)}, bf16[2,64,512]{2,1,0:T(8,128)(2,1)S(1)}, u32[]{:S(2)}, u32[]{:S(2)}) collective-permute-start(bf16[2,64,512]{2,1,0:T(8,128)(2,1)S(1)} %get-tuple-element.31), channel_id=1, source_target_pairs={{0,1},{1,0},{2,3},{3,2},{4,5},{5,4},{6,7},{7,6},{8,9},{9,8},{10,11... | collective-permute-start | bytes 393224 | tf_op jit(solution)/shard_map/ppermute | solution.py:248
  27.7 8.0 %collective-permute-start.13 = (bf16[2,64,512]{2,1,0:T(8,128)(2,1)S(1)}, bf16[2,64,512]{2,1,0:T(8,128)(2,1)S(1)}, u32[]{:S(2)}, u32[]{:S(2)}) collective-permute-start(bf16[2,64,512]{2,1,0:T(8,128)(2,1)S(1)} %get-tuple-element.28), channel_id=1, source_target_pairs={{0,1},{1,0},{2,3},{3,2},{4,5},{5,4},{6,7},{7,6},{8,9},{9,8},{10,11... | collective-permute-start | bytes 393224 | tf_op jit(solution)/shard_map/ppermute | solution.py:248
  27.9 15.5 %copy-start.4 = (bf16[32,512,128]{2,1,0:T(8,128)(2,1)S(1)}, bf16[32,512,128]{2,1,0:T(8,128)(2,1)}, u32[]{:S(2)}) copy-start(bf16[32,512,128]{2,1,0:T(8,128)(2,1)} %param.12) | copy-start | bytes 12582916
  32.0 5.3 %collective-permute-start.11 = (bf16[4,64,512]{2,1,0:T(8,128)(2,1)S(1)}, bf16[4,64,512]{2,1,0:T(8,128)(2,1)S(1)}, u32[]{:S(2)}, u32[]{:S(2)}) collective-permute-start(bf16[4,64,512]{2,1,0:T(8,128)(2,1)S(1)} %get-tuple-element.24), channel_id=1, source_target_pairs={{0,1},{1,0},{2,3},{3,2},{4,5},{5,4},{6,7},{7,6},{8,9},{9,8},{10,11... | collective-permute-start | bytes 786440 | tf_op jit(solution)/shard_map/ppermute | solution.py:248
  32.3 1.2 %collective-permute-start.17 = (f32[2,1,64]{2,1,0:T(1,128)S(1)}, f32[2,1,64]{2,1,0:T(1,128)S(1)}, u32[]{:S(2)}, u32[]{:S(2)}) collective-permute-start(f32[2,1,64]{2,1,0:T(1,128)S(1)} %get-tuple-element.32), channel_id=1, source_target_pairs={{0,1},{1,0},{2,3},{3,2},{4,5},{5,4},{6,7},{7,6},{8,9},{9,8},{10,11... | collective-permute-start | bytes 1544 | tf_op jit(solution)/shard_map/ppermute | solution.py:248
  32.5 3.3 %collective-permute-start.14 = (f32[2,1,64]{2,1,0:T(1,128)S(1)}, f32[2,1,64]{2,1,0:T(1,128)S(1)}, u32[]{:S(2)}, u32[]{:S(2)}) collective-permute-start(f32[2,1,64]{2,1,0:T(1,128)S(1)} %get-tuple-element.29), channel_id=1, source_target_pairs={{0,1},{1,0},{2,3},{3,2},{4,5},{5,4},{6,7},{7,6},{8,9},{9,8},{10,11... | collective-permute-start | bytes 1544 | tf_op jit(solution)/shard_map/ppermute | solution.py:248
  33.7 6.6 %collective-permute-start.18 = (bf16[136,512]{1,0:T(8,128)(2,1)S(1)}, bf16[136,512]{1,0:T(8,128)(2,1)S(1)}, u32[]{:S(2)}, u32[]{:S(2)}) collective-permute-start(bf16[136,512]{1,0:T(8,128)(2,1)S(1)} %weigh.3), channel_id=1, source_target_pairs={{0,2},{1,3},{2,0},{3,1},{4,6},{5,7},{6,4},{7,5},{8,10},{9,11},{10,... | collective-permute-start | bytes 417800 | tf_op jit(solution)/shard_map/ppermute | solution.py:248
  35.9 7.0 %collective-permute-start.15 = (bf16[136,512]{1,0:T(8,128)(2,1)S(1)}, bf16[136,512]{1,0:T(8,128)(2,1)S(1)}, u32[]{:S(2)}, u32[]{:S(2)}) collective-permute-start(bf16[136,512]{1,0:T(8,128)(2,1)S(1)} %weigh.2), channel_id=1, source_target_pairs={{0,2},{1,3},{2,0},{3,1},{4,6},{5,7},{6,4},{7,5},{8,10},{9,11},{10,... | collective-permute-start | bytes 417800 | tf_op jit(solution)/shard_map/ppermute | solution.py:248
  36.0 1.2 %collective-permute-start.12 = (f32[4,1,64]{2,1,0:T(1,128)S(1)}, f32[4,1,64]{2,1,0:T(1,128)S(1)}, u32[]{:S(2)}, u32[]{:S(2)}) collective-permute-start(f32[4,1,64]{2,1,0:T(1,128)S(1)} %get-tuple-element.26), channel_id=1, source_target_pairs={{0,1},{1,0},{2,3},{3,2},{4,5},{5,4},{6,7},{7,6},{8,9},{9,8},{10,11... | collective-permute-start | bytes 3080 | tf_op jit(solution)/shard_map/ppermute | solution.py:248
